TPU v7x, 128 devices: a whole 4x4x4 slice. The times are simulated.
128 devices in a mesh: group: 8 (over x, core), slab: 16 (over z, y).
Axes of the slice: x: 4, y: 4, z: 4, core: 2. Of those that a mesh axis runs over, the one named last changes fastest.
Arguments:
- initial_samples: float32 [96, 128, 4096], P('group', 'slab'), may hold values from -6 to 6
- transport_ratios: float32 [3, 128, 4096], P(None, 'slab'), may hold values from 0.05 to 0.33
- assignment: int32 [96], replicated, may hold values from 0 to 95, each once
- obs_values: float32 [512, 512], P(('group', 'slab')), may hold values from -6 to 6
- obs_error: float32 [512, 512], P(('group', 'slab')), may hold values from 0.25 to 4
- sensor_easting_offset: int32 [512, 512], P(('group', 'slab')), may hold values from 0 to 127
- obs_column: int32 [512, 512], P(('group', 'slab')), may hold values from 0 to 23
- obs_count: int32 [512], P(('group', 'slab')), may hold values from 1 to 512, 131072 in all
Outputs:
- analysis: float32 [96, 128, 4096], P('group', 'slab')
Inputs may be any that keep to these rules, and one draw needn't show every extreme that they name: `assignment`: a permutation of the members. A block's live observations are its first obs_count entries; some block has exactly 512.
All inputs are finite; a program needn't handle non-finite values.
Results may differ from a plain program's by a relative error of at most 0.0003.
Values sent between devices are 32-bit elements; how exact they have to be, the bound alone decides.
A program may use at most 64 MiB of HBM per device.

v0:
```python
import jax
import jax.numpy as jnp
from jax import lax
from jax.sharding import PartitionSpec as P

MEMBERS = 96
NZ = 64
STEPS = 6
TILE_WIDTH = 8
HC = 8
OBS = 512
ITERS = 8


def shifted(block, axis, distance):
    devices = range(lax.axis_size(axis))
    route = [((i - distance) % len(devices), i) for i in devices]
    return lax.ppermute(block, axis, route)


def split_up(x, dim, length):
    before, after = (x.shape[:dim], x.shape[dim + 1 :])
    return jnp.moveaxis(x.reshape(*before, length, -1, *after), dim, 0)


def joined_along(pieces, dim):
    shape = list(pieces.shape[1:])
    shape[dim] *= pieces.shape[0]
    return jnp.moveaxis(pieces, 0, dim).reshape(shape)


def joined_exchange(x, axis, axes, splits, concats):
    sizes = [lax.axis_size(a) for a in axes]
    pieces = split_up(x, splits[0], sizes[0])
    pieces = jnp.moveaxis(split_up(pieces, splits[1] + 1, sizes[1]), 0, 1)
    inside = pieces.shape[2:]
    pieces = pieces.reshape(-1, *inside)
    pieces = lax.all_to_all(pieces, axis, split_axis=0, concat_axis=0, tiled=True)
    pieces = joined_along(pieces.reshape(*sizes, *inside), concats[0] + 1)
    return joined_along(pieces, concats[1])


def with_halo(x, sides, width):
    edges = {}
    for axis, dim in sides:
        size, length = (lax.axis_size(axis), x.shape[dim])
        up = [(i, (i + 1) % size) for i in range(size)]
        last = lax.slice_in_dim(x, length - width, length, axis=dim)
        first = lax.slice_in_dim(x, 0, width, axis=dim)
        edges[dim] = (
            lax.ppermute(last, axis, up),
            lax.ppermute(first, axis, [(b, a) for a, b in up]),
        )
    done = []
    for _, dim in sides:
        low, high = edges[dim]
        around = [(width, width) if d in done else (0, 0) for d in range(x.ndim)]
        x = jnp.concatenate([jnp.pad(low, around), x, jnp.pad(high, around)], axis=dim)
        done.append(dim)
    return x


def advance(sample_state, upwind, rates):
    z_position = jnp.arange(sample_state.shape[2]) % NZ
    below_y = jnp.roll(sample_state, NZ, axis=2)
    below_z = jnp.where(
        z_position == 0, jnp.roll(sample_state, 1 - NZ, axis=2), jnp.roll(sample_state, 1, axis=2)
    )
    return (
        sample_state
        - rates[0] * (sample_state - upwind)
        - rates[1] * (sample_state - below_y)
        - rates[2] * (sample_state - below_z)
    )


def shards(
    initial_samples,
    transport_ratios,
    assignment,
    obs_values,
    obs_error,
    sensor_easting_offset,
    obs_column,
    obs_count,
):
    hi = lax.Precision.HIGHEST
    local_members, planes, total_columns = initial_samples.shape
    group_count = lax.axis_size("group")
    slab_count = lax.axis_size("slab")
    own_columns = total_columns // (group_count * slab_count)
    edge_state, edge_rates = shifted(
        (initial_samples[:, planes - STEPS :], transport_ratios[:, planes - STEPS :]), "slab", 1
    )
    state = jnp.concatenate([edge_state, initial_samples], axis=1)
    rates = jnp.concatenate([edge_rates, transport_ratios], axis=1)
    for section in range(STEPS):
        state = advance(state[:, 1:], state[:, :-1], rates[:, section + 1 :])
    vertical_line_positions = joined_exchange(
        state, ("group", "slab"), ("group", "slab"), (2, 2), (0, 1)
    )
    grid_x = vertical_line_positions.shape[1]
    own_blocks = obs_values.shape[0]
    block_start = (TILE_WIDTH * jnp.arange(own_blocks, dtype=jnp.int32))[:, None]
    edge_blocks = (HC + TILE_WIDTH - 1) // TILE_WIDTH
    window_col = block_start - HC + obs_column
    requests = jnp.stack([sensor_easting_offset, obs_column])
    asked = with_halo(requests, ((("group", "slab"), 1),), edge_blocks)
    left_asked = asked[:, :edge_blocks]
    right_asked = asked[:, edge_blocks + own_blocks :]
    edge_index = jnp.arange(edge_blocks, dtype=jnp.int32)[:, None]
    left_cols = (
        TILE_WIDTH * (own_blocks - edge_blocks + edge_index) - HC + left_asked[1] - own_columns
    )
    right_cols = TILE_WIDTH * edge_index - HC + right_asked[1] + own_columns
    serve_level = jnp.concatenate([left_asked[0], right_asked[0]], axis=0)
    serve_cols = jnp.clip(jnp.concatenate([left_cols, right_cols], axis=0), 0, own_columns - 1)
    flattened = vertical_line_positions.reshape(MEMBERS, grid_x * own_columns)
    serve_pos = (serve_level * own_columns + serve_cols).reshape(-1)
    served = jnp.take(flattened, serve_pos, axis=1).reshape(MEMBERS, 2 * edge_blocks, OBS)
    answered = with_halo(served, ((("group", "slab"), 1),), edge_blocks)
    from_left = answered[:, :edge_blocks]
    from_right = answered[:, 3 * edge_blocks :]
    filler = jnp.zeros((MEMBERS, own_blocks - edge_blocks, OBS), jnp.float32)
    left_full = jnp.concatenate([from_left, filler], axis=1)
    right_full = jnp.concatenate([filler, from_right], axis=1)
    local_pos = (
        sensor_easting_offset * own_columns + jnp.clip(window_col, 0, own_columns - 1)
    ).reshape(-1)
    local_vals = jnp.take(flattened, local_pos, axis=1).reshape(MEMBERS, own_blocks, OBS)
    modelled_readings = jnp.where(
        window_col[None] < 0,
        left_full,
        jnp.where(window_col[None] >= own_columns, right_full, local_vals),
    )
    slots = jnp.arange(OBS, dtype=jnp.int32)[None, :]
    pred_mean = jnp.mean(modelled_readings, axis=0)
    weight = jnp.where(slots < obs_count[:, None], 1.0 / jnp.sqrt(obs_error * (MEMBERS - 1.0)), 0.0)
    scaled = jnp.transpose((modelled_readings - pred_mean[None]) * weight[None], (1, 0, 2))
    innovation = (obs_values - pred_mean) * weight
    identity = jnp.eye(MEMBERS, dtype=jnp.float32)
    gram = identity[None] + jnp.einsum("bmk,bnk->bmn", scaled, scaled, precision=hi)
    fro_norm = jnp.sqrt(jnp.sum(gram * gram, axis=(1, 2)))
    iterate_a = gram / fro_norm[:, None, None]
    iterate_z = jnp.broadcast_to(identity, gram.shape)
    for iteration in range(ITERS):
        middle = 1.5 * identity[None] - 0.5 * jnp.einsum(
            "bij,bjk->bik", iterate_z, iterate_a, precision=hi
        )
        iterate_a = jnp.einsum("bij,bjk->bik", iterate_a, middle, precision=hi)
        iterate_z = jnp.einsum("bij,bjk->bik", middle, iterate_z, precision=hi)
    transform = iterate_z / jnp.sqrt(fro_norm)[:, None, None]
    projected = jnp.einsum("bmk,bk->bm", scaled, innovation, precision=hi)
    inner_step = jnp.einsum("bmn,bn->bm", transform, projected, precision=hi)
    mean_weights = jnp.einsum("bmn,bn->bm", transform, inner_step, precision=hi)
    weights_all = mean_weights[:, :, None] + transform
    one_hot = (assignment[:, None] == jnp.arange(MEMBERS, dtype=jnp.int32)[None, :]).astype(
        jnp.float32
    )
    ordered = jnp.einsum("bmn,nj->bmj", weights_all, one_hot, precision=hi)
    column_weights = jnp.repeat(ordered, TILE_WIDTH, axis=0)
    column_major = jnp.transpose(vertical_line_positions, (2, 0, 1))
    cell_mean = jnp.mean(column_major, axis=1)
    updated = cell_mean[:, None, :] + jnp.einsum(
        "cmj,cmx->cjx", column_weights, column_major - cell_mean[:, None, :], precision=hi
    )
    analysed = jnp.transpose(updated, (1, 2, 0))
    outgoing = analysed.reshape(MEMBERS, grid_x, 1, own_columns)
    returned = joined_exchange(outgoing, ("group", "slab"), ("group", "slab"), (0, 1), (2, 3))
    result = returned.reshape(local_members, planes, total_columns)
    return result


def solution(mesh):
    placed = (
        P("group", "slab", None),
        P(None, "slab", None),
        P(),
        P(("group", "slab"), None),
        P(("group", "slab"), None),
        P(("group", "slab"), None),
        P(("group", "slab"), None),
        P(("group", "slab")),
    )
    return jax.shard_map(
        shards, mesh=mesh, in_specs=placed, out_specs=P("group", "slab", None), check_vma=False
    )
```

profile of v0, /device:TPU:1, one launch (start us, length us, event | category | flops | bytes accessed | tf_op | source)
XLA Modules:
  0.0 254.7 jit_solution(8528914998588665176)
XLA Ops:
  7.3 4.1 %collective-permute-start.3 = (s32[2,1,512]{2,1,0:T(1,128)S(1)}, s32[2,1,512]{2,1,0:T(1,128)S(1)}, u32[]{:S(2)}, u32[]{:S(2)}) collective-permute-start(s32[2,1,512]{2,1,0:T(1,128)S(1)} %get-tuple-element.32), channel_id=1, source_target_pairs={{1,0},{2,1},{3,2},{4,3},{5,4},{6,5},{7,6},{8,7},{9,8},{10,9},{11,1... | collective-permute-start | bytes 12296 | tf_op jit(solution)/shard_map/ppermute | solution.py:52
  12.2 4.9 %collective-permute-done.1 = f32[3,6,4096]{2,1,0:T(8,128)S(1)} collective-permute-done((f32[3,6,4096]{2,1,0:T(8,128)S(1)}, f32[3,6,4096]{2,1,0:T(8,128)S(1)}, u32[]{:S(2)}, u32[]{:S(2)}) %collective-permute-start.1) | collective-permute-done | bytes 294944 | tf_op jit(solution)/shard_map/ppermute | solution.py:18
  17.7 33.1 %collective-permute-done = f32[12,6,4096]{2,1,0:T(8,128)S(1)} collective-permute-done((f32[12,6,4096]{2,1,0:T(8,128)S(1)}, f32[12,6,4096]{2,1,0:T(8,128)S(1)}, u32[]{:S(2)}, u32[]{:S(2)}) %collective-permute-start) | collective-permute-done | bytes 1179680 | tf_op jit(solution)/shard_map/ppermute | solution.py:18
  52.9 4.4 %fusion.6 = f32[12,13,4096]{2,1,0:T(8,128)S(1)} fusion(f32[12,6,4096]{2,1,0:T(8,128)S(1)} %collective-permute-done, f32[12,8,4096]{2,1,0:T(8,128)S(1)} %copy-done, f32[12,13,4032]{2,1,0:T(8,128)S(1)} %fusion.7, f32[12,13,64]{2,1,0:T(8,128)S(1)} %fusion.99, f32[12,13,63]{2,1,0:T(8,128)S(1)} %fusion.100, f32[12,13,4033]{2,1,0:T(8,128)S(1)} %fusion.8, ...), kind=kLoop, calls=%fused_computation.22 | loop fusion | flops 10223616 | bytes 11063920 | tf_op jit(solution)/shard_map/sub | solution.py:70
  79.6 3.8 %reshape.198 = f32[8,12,8,16,32]{4,3,2,1,0:T(8,128)} reshape(f32[8,12,8,512]{3,2,1,0:T(8,128)S(1)} %bitcast.189) | data formatting | bytes 3145728 | tf_op jit(solution)/shard_map/reshape | solution.py:23
  83.4 7.3 %copy.38 = f32[8,16,12,8,32]{4,3,2,1,0:T(8,128)} copy(f32[8,16,12,8,32]{4,1,3,2,0:T(8,128)} %bitcast.181) | data formatting | bytes 3145728 | tf_op jit(solution)/shard_map/transpose;transpose | solution.py:35
  90.7 6.0 %reshape.231 = f32[128,1,3072]{2,1,0:T(1,128)} reshape(f32[128,12,8,32]{3,2,1,0:T(8,128)} %bitcast.182) | data formatting | bytes 3145728
  96.8 7.0 %all-to-all-start = ((f32[128,1,3072]{2,1,0:T(1,128)}), f32[128,1,3072]{2,1,0:T(1,128)S(1)}, u32[]{:S(2)}, u32[]{:S(2)}) async-start(f32[128,1,3072]{2,1,0:T(1,128)} %reshape.231), calls=%async_computation | async-start | bytes 3145728 | tf_op jit(solution)/shard_map/all_to_all | solution.py:38
  104.0 23.7 %all-to-all-done = f32[128,1,3072]{2,1,0:T(1,128)S(1)} async-done(((f32[128,1,3072]{2,1,0:T(1,128)}), f32[128,1,3072]{2,1,0:T(1,128)S(1)}, u32[]{:S(2)}, u32[]{:S(2)}) %all-to-all-start) | async-done | bytes 1572896 | tf_op jit(solution)/shard_map/all_to_all | solution.py:38
  128.3 4.3 %reduce = f32[128,3072]{1,0:T(8,128)S(1)} reduce(f32[128,1,3072]{2,1,0:T(1,128)S(1)} %all-to-all-done, f32[]{:T(128)} %broadcast.222), dimensions={1}, to_apply=%all_to_all.6.reduce_sub_computation | reduce | bytes 3145732 | tf_op jit(solution)/shard_map/all_to_all | solution.py:38
  132.6 3.8 %reshape.232 = f32[128,12,8,32]{3,2,1,0:T(8,128)} reshape(f32[128,3072]{1,0:T(8,128)S(1)} %reduce) | data formatting | bytes 3145728
  136.4 6.0 %copy.39 = f32[16,8,12,8,32]{4,3,2,1,0:T(8,128)} copy(f32[16,8,12,8,32]{4,3,2,0,1:T(8,128)} %bitcast.183) | data formatting | bytes 3145728 | tf_op jit(solution)/shard_map/transpose | solution.py:29
  142.4 4.5 %copy.40 = f32[96,16,8,32]{0,3,2,1:T(8,128)S(1)} copy(f32[96,16,8,32]{3,2,0,1:T(8,128)} %bitcast.180) | data formatting | bytes 3145728 | tf_op jit(solution)/shard_map/transpose | solution.py:29
  152.3 4.2 %collective-permute-start.5 = (f32[96,1,512]{2,0,1:T(8,128)}, f32[96,1,512]{2,0,1:T(8,128)}, u32[]{:S(2)}, u32[]{:S(2)}) collective-permute-start(f32[96,1,512]{2,0,1:T(8,128)} %get-tuple-element.25), channel_id=1, source_target_pairs={{1,0},{2,1},{3,2},{4,3},{5,4},{6,5},{7,6},{8,7},{9,8},{10,9},{11,1... | collective-permute-start | bytes 589832 | tf_op jit(solution)/shard_map/ppermute | solution.py:52
  156.5 5.6 %gather_fusion.1 = f32[2048,96]{1,0:T(8,128)S(1)} fusion(f32[96,4096]{0,1:T(8,128)S(1)} %bitcast.179, s32[2048]{0:T(1024)S(1)} %broadcast_clamp_fusion), kind=kCustom, calls=%fused_computation.1 | custom fusion | bytes 1581056 | tf_op jit(solution)/shard_map/jit(_take)/gather | solution.py:130
  179.1 5.5 %bitcast_add_fusion = f32[96,128,32]{1,0,2:T(8,128)S(1)} fusion(f32[32,96,96]{1,2,0:T(8,128)S(1)} %bitcast.188, f32[32,96,128]{1,0,2:T(8,128)S(1)} %broadcast_subtract_fusion, f32[128,32]{0,1:T(8,128)S(1)} %copy.41), kind=kOutput, calls=%fused_computation.112 | convolution fusion | flops 453378048 | bytes 4341760 | tf_op jit(solution)/shard_map/cmj,cmx->cjx/dot_general | solution.py:164
  184.6 4.0 %copy.47 = f32[96,128,32]{2,1,0:T(8,128)} copy(f32[96,128,32]{1,0,2:T(8,128)S(1)} %bitcast_add_fusion) | data formatting | bytes 3145728 | tf_op jit(solution)/shard_map/add | solution.py:164
  188.6 6.2 %copy.48 = f32[8,16,12,8,1,32]{5,3,2,1,0,4:T(8,128)} copy(f32[8,16,12,8,1,32]{5,3,1,2,0,4:T(8,128)} %bitcast.184) | data formatting | bytes 3145728 | tf_op jit(solution)/shard_map/transpose;transpose | solution.py:35
  194.9 5.2 %reshape.233 = f32[128,1,3072]{2,1,0:T(1,128)S(1)} reshape(f32[128,1,12,8,32]{4,3,2,1,0:T(8,128)} %bitcast.185) | data formatting | bytes 3145728
  200.0 31.1 %all_to_all.10 = f32[128,1,3072]{2,1,0:T(1,128)S(1)} all-to-all(f32[128,1,3072]{2,1,0:T(1,128)S(1)} %reshape.233), channel_id=1, replica_groups=mesh['group'=8,'slab'=16] {'group','slab'}, dimensions={0} | all-to-all | bytes 3145728 | tf_op jit(solution)/shard_map/all_to_all | solution.py:38
  231.2 4.3 %reduce.1 = f32[128,3072]{1,0:T(8,128)S(1)} reduce(f32[128,1,3072]{2,1,0:T(1,128)S(1)} %all_to_all.10, f32[]{:T(128)} %broadcast.222), dimensions={1}, to_apply=%all_to_all.7.reduce_sub_computation | reduce | bytes 3145732 | tf_op jit(solution)/shard_map/all_to_all | solution.py:38
  235.5 3.8 %reshape.234 = f32[128,1,12,8,32]{4,3,2,1,0:T(8,128)} reshape(f32[128,3072]{1,0:T(8,128)S(1)} %reduce.1) | data formatting | bytes 3145728
  239.3 9.0 %copy.50 = f32[12,8,8,16,32]{4,3,2,1,0:T(8,128)} copy(f32[12,8,8,16,32]{4,1,0,3,2:T(8,128)} %bitcast.186) | data formatting | bytes 3145728 | tf_op jit(solution)/shard_map/transpose | solution.py:29
  248.4 6.1 %reshape_reshape.7 = f32[12,8,4096]{2,1,0:T(8,128)} reshape(f32[12,8,8,16,32]{4,3,2,1,0:T(8,128)} %copy.50) | data formatting | bytes 3145728 | tf_op jit(solution)/shard_map/reshape;reshape | solution.py:170
  (135 shorter events, 55.4 us)
Async XLA Ops:
  0.0 11.4 %copy-start.1 = (f32[3,8,4096]{2,1,0:T(8,128)S(1)}, f32[3,8,4096]{2,1,0:T(8,128)}, u32[]{:S(2)}) copy-start(f32[3,8,4096]{2,1,0:T(8,128)} %param.9) | copy-start | bytes 1179652
  0.0 6.2 %copy-start.5 = (s32[4,512]{1,0:T(4,128)S(1)}, s32[4,512]{1,0:T(4,128)}, u32[]{:S(2)}) copy-start(s32[4,512]{1,0:T(4,128)} %param.13) | copy-start | bytes 24580
  0.0 6.2 %copy-start.4 = (s32[4,512]{1,0:T(4,128)S(1)}, s32[4,512]{1,0:T(4,128)}, u32[]{:S(2)}) copy-start(s32[4,512]{1,0:T(4,128)} %param.14) | copy-start | bytes 24580
  1.1 16.0 %collective-permute-start.1 = (f32[3,6,4096]{2,1,0:T(8,128)S(1)}, f32[3,6,4096]{2,1,0:T(8,128)S(1)}, u32[]{:S(2)}, u32[]{:S(2)}) collective-permute-start(f32[3,6,4096]{2,1,0:T(8,128)S(1)} %slice.322), channel_id=1, source_target_pairs={{15,0},{0,1},{1,2},{2,3},{3,4},{4,5},{5,6},{6,7},{7,8},{8,9},{9,10... | collective-permute-start | bytes 884744 | tf_op jit(solution)/shard_map/ppermute | solution.py:18
  4.9 45.9 %collective-permute-start = (f32[12,6,4096]{2,1,0:T(8,128)S(1)}, f32[12,6,4096]{2,1,0:T(8,128)S(1)}, u32[]{:S(2)}, u32[]{:S(2)}) collective-permute-start(f32[12,6,4096]{2,1,0:T(8,128)S(1)} %slice.320), channel_id=1, source_target_pairs={{15,0},{0,1},{1,2},{2,3},{3,4},{4,5},{5,6},{6,7},{7,8},{8,9},{9,10... | collective-permute-start | bytes 3538952 | tf_op jit(solution)/shard_map/ppermute | solution.py:18
  6.3 97.6 %collective-permute-start.2 = (s32[2,1,512]{2,1,0:T(1,128)S(1)}, s32[2,1,512]{2,1,0:T(1,128)S(1)}, u32[]{:S(2)}, u32[]{:S(2)}) collective-permute-start(s32[2,1,512]{2,1,0:T(1,128)S(1)} %get-tuple-element.31), channel_id=1, source_target_pairs={{0,1},{1,2},{2,3},{3,4},{4,5},{5,6},{6,7},{7,8},{8,9},{9,10},{10,1... | collective-permute-start | bytes 12296 | tf_op jit(solution)/shard_map/ppermute | solution.py:51
  7.3 96.6 %collective-permute-start.3 = (s32[2,1,512]{2,1,0:T(1,128)S(1)}, s32[2,1,512]{2,1,0:T(1,128)S(1)}, u32[]{:S(2)}, u32[]{:S(2)}) collective-permute-start(s32[2,1,512]{2,1,0:T(1,128)S(1)} %get-tuple-element.32), channel_id=1, source_target_pairs={{1,0},{2,1},{3,2},{4,3},{5,4},{6,5},{7,6},{8,7},{9,8},{10,9},{11,1... | collective-permute-start | bytes 12296 | tf_op jit(solution)/shard_map/ppermute | solution.py:52
  17.2 33.6 %copy-start = (f32[12,8,4096]{2,1,0:T(8,128)S(1)}, f32[12,8,4096]{2,1,0:T(8,128)}, u32[]{:S(2)}) copy-start(f32[12,8,4096]{2,1,0:T(8,128)} %param.8) | copy-start | bytes 4718596
  96.8 31.0 %all-to-all-start = ((f32[128,1,3072]{2,1,0:T(1,128)}), f32[128,1,3072]{2,1,0:T(1,128)S(1)}, u32[]{:S(2)}, u32[]{:S(2)}) async-start(f32[128,1,3072]{2,1,0:T(1,128)} %reshape.231), calls=%async_computation | async-start | bytes 3145728 | tf_op jit(solution)/shard_map/all_to_all | solution.py:38
  151.4 12.6 %collective-permute-start.4 = (f32[96,1,512]{2,0,1:T(8,128)}, f32[96,1,512]{2,0,1:T(8,128)S(1)}, u32[]{:S(2)}, u32[]{:S(2)}) collective-permute-start(f32[96,1,512]{2,0,1:T(8,128)} %get-tuple-element.24), channel_id=1, source_target_pairs={{0,1},{1,2},{2,3},{3,4},{4,5},{5,6},{6,7},{7,8},{8,9},{9,10},{10,1... | collective-permute-start | bytes 589832 | tf_op jit(solution)/shard_map/ppermute | solution.py:51
  152.3 11.8 %collective-permute-start.5 = (f32[96,1,512]{2,0,1:T(8,128)}, f32[96,1,512]{2,0,1:T(8,128)}, u32[]{:S(2)}, u32[]{:S(2)}) collective-permute-start(f32[96,1,512]{2,0,1:T(8,128)} %get-tuple-element.25), channel_id=1, source_target_pairs={{1,0},{2,1},{3,2},{4,3},{5,4},{6,5},{7,6},{8,7},{9,8},{10,9},{11,1... | collective-permute-start | bytes 589832 | tf_op jit(solution)/shard_map/ppermute | solution.py:52
  163.3 1.1 copy-start.2
  163.3 2.2 copy-start.6
  163.4 2.2 copy-start.7
  163.4 2.2 copy-start.8
  163.4 2.3 copy-start.3
  173.7 4.7 %copy-start.9 = (s32[96]{0:T(128)S(1)}, s32[96]{0:T(128)}, u32[]{:S(2)}) copy-start(s32[96]{0:T(128)} %param.10) | copy-start | bytes 1156
where the time goes:
time: 259 us; the launch traced here: 255 us
  local copies, waits for them, and re-layouts  88.9 us (34%)
  waiting for transfers between devices  61.8 us (24%)
  other arithmetic  32.5 us (13%)
  blocking collectives  31.1 us (12%)
  starting transfers between devices  20.8 us (8%)
  matrix products  18.5 us (7%)
    ppermute x2, waiting for transfers between devices, shifted(): return lax.ppermute(block, axis, route)  38 us
    all_to_all x1, blocking collectives, joined_exchange(): lax.all_to_all(pieces, axis, split_axis=0, concat_axis=0, tiled=True)  31.1 us
    all_to_all x1, waiting for transfers between devices, joined_exchange(): lax.all_to_all(pieces, axis, split_axis=0, concat_axis=0, tiled=True)  23.7 us
    transpose x3, local copies, waits for them, and re-layouts, joined_along(): return jnp.moveaxis(pieces, 0, dim).reshape(shape)  19.6 us
    unnamed x26, local copies, waits for them, and re-layouts  19.2 us
    sub x6, other arithmetic, advance(): sample_state - rates[0] * (sample_state - upwind)  17.9 us
    another operation x2, local copies, waits for them, and re-layouts, joined_exchange(): pieces = jnp.moveaxis(split_up(pieces, splits[1] + 1, sizes[1]), 0, 1)  13.5 us
    all_to_all x2, other arithmetic, joined_exchange(): lax.all_to_all(pieces, axis, split_axis=0, concat_axis=0, tiled=True)  8.69 us
  transfers between devices with their start and end apart: 7, of which 3 were waited for; matrix products, arithmetic and copies ran while one was open for 22% of the time, Pallas kernels for 0%

commit v1 on v0

v1 whole, which is shorter than its diff:
```python
import jax
import jax.numpy as jnp
from jax import lax
from jax.experimental import pallas as pl
from jax.experimental.pallas import tpu as pltpu
from jax.sharding import PartitionSpec as P

MEMBERS = 96
NZ = 64
STEPS = 6
TILE_WIDTH = 8
HC = 8
OBS = 512
ITERS = 8

GROUPS = 8
SLABS = 16
DEVICES = GROUPS * SLABS
PLANES = 8
TILES = 32
LANES = 128
QUADS = 3
OWN = 32
BLOCKS = 4
CELLS = PLANES * OWN
ROWS = 112
MESH = pl.DeviceIdType.MESH


def nt(a, b):
    return lax.dot_general(a, b, (((1,), (1,)), ((), ())), preferred_element_type=jnp.float32)


def nn(a, b):
    return lax.dot_general(a, b, (((1,), (0,)), ((), ())), preferred_element_type=jnp.float32)


def halves(a):
    high = a.astype(jnp.bfloat16)
    return high, (a - high.astype(jnp.float32)).astype(jnp.bfloat16)


def product(a, b):
    m = a.shape[0]
    ah, al = halves(a)
    bh, bl = halves(b)
    both = nn(jnp.concatenate([ah, al], axis=0), jnp.concatenate([bh, bl], axis=1))
    return both[:m, :LANES] + (both[:m, LANES:] + both[m:, :LANES])


def swap_rows(tiles, row):
    axis = tiles[0].ndim - 2
    t0, t1, t2, t3 = tiles
    up = (row & 2) == 0
    b0 = jnp.where(up, t0, pltpu.roll(t2, 2, axis))
    b2 = jnp.where(up, pltpu.roll(t0, 6, axis), t2)
    b1 = jnp.where(up, t1, pltpu.roll(t3, 2, axis))
    b3 = jnp.where(up, pltpu.roll(t1, 6, axis), t3)
    even = (row & 1) == 0
    o0 = jnp.where(even, b0, pltpu.roll(b1, 1, axis))
    o1 = jnp.where(even, pltpu.roll(b0, 7, axis), b1)
    o2 = jnp.where(even, b2, pltpu.roll(b3, 1, axis))
    o3 = jnp.where(even, pltpu.roll(b2, 7, axis), b3)
    return o0, o1, o2, o3


def swap_lanes(tiles, lane):
    axis = tiles[0].ndim - 1
    t0, t1, t2, t3 = tiles
    low = (lane & 64) == 0
    b0 = jnp.where(low, t0, pltpu.roll(t2, 64, axis))
    b2 = jnp.where(low, pltpu.roll(t0, 64, axis), t2)
    b1 = jnp.where(low, t1, pltpu.roll(t3, 64, axis))
    b3 = jnp.where(low, pltpu.roll(t1, 64, axis), t3)
    even = (lane & 32) == 0
    o0 = jnp.where(even, b0, pltpu.roll(b1, 32, axis))
    o1 = jnp.where(even, pltpu.roll(b0, 96, axis), b1)
    o2 = jnp.where(even, b2, pltpu.roll(b3, 32, axis))
    o3 = jnp.where(even, pltpu.roll(b2, 96, axis), b3)
    return o0, o1, o2, o3


def iota(shape, dim):
    return lax.broadcasted_iota(jnp.int32, shape, dim)


def kernel(
    x_ref,
    c_ref,
    asg_ref,
    val_ref,
    err_ref,
    east_ref,
    col_ref,
    cnt_ref,
    o_ref,
    state,
    halo_out,
    halo_in,
    outgoing,
    incoming,
    returned,
    split,
    mean_of,
    maps,
    edge_out,
    edge_in,
    acc,
    part_in,
    select,
    ordered,
    halo_send,
    halo_recv,
    edge_send,
    edge_recv,
    part_send,
    part_recv,
    send_sem,
    recv_sem,
    back_send,
    back_recv,
):
    g = lax.axis_index("group")
    s = lax.axis_index("slab")
    me = g * SLABS + s

    def place(d):
        return (d // SLABS, d % SLABS)

    left = place((me + DEVICES - 1) % DEVICES)
    right = place((me + 1) % DEVICES)

    barrier = pltpu.get_barrier_semaphore()

    def greet(i, carry):
        pl.semaphore_signal(
            barrier, inc=1, device_id=place((me + i) % DEVICES), device_id_type=MESH
        )
        return carry

    lax.fori_loop(1, DEVICES, greet, 0)

    row = iota((4, 8, LANES), 1)
    lane = iota((4, 8, LANES), 2)
    first_row = row == 0
    low_half = lane < 64
    z_first = (lane & (NZ - 1)) == 0

    def advance(u, above, carried, tile):
        turned = pltpu.roll(u, 64, 2)
        below_y = jnp.where(low_half, carried, turned)
        below_z = jnp.where(z_first, pltpu.roll(turned, 1, 2), pltpu.roll(u, 1, 2))
        new = (
            u
            - c_ref[0, tile] * (u - above)
            - c_ref[1, tile] * (u - below_y)
            - c_ref[2, tile] * (u - below_z)
        )
        return new, turned

    def source(quad, level):
        if level == 0:
            return lambda tile: x_ref[pl.ds(4 * quad, 4), tile]
        return lambda tile: state[level % 2, tile]

    def levels_of(quad):
        for level in range(STEPS - 1):
            read = source(quad, level)

            def one(tile, carried, level=level, read=read):
                u = read(tile)
                if level == 0:
                    for i in range(4):
                        halo_out[quad, tile, 6 * i : 6 * i + 1] = u[i, 7:8]
                new, turned = advance(u, pltpu.roll(u, 1, 1), carried, tile)
                if level < STEPS - 2:
                    state[(level + 1) % 2, tile] = new
                for i in range(4):
                    at = 6 * i + level + 1
                    halo_out[quad, tile, at : at + 1] = new[i, 7:8]
                return turned

            lax.fori_loop(0, TILES, one, pltpu.roll(read(TILES - 1), 64, 2), unroll=4)

    next_slab = (g, (s + 1) % SLABS)

    def halo_copy(quad):
        return pltpu.make_async_remote_copy(
            src_ref=halo_out.at[quad],
            dst_ref=halo_in.at[quad],
            send_sem=halo_send.at[quad],
            recv_sem=halo_recv.at[quad],
            device_id=next_slab,
            device_id_type=MESH,
        )

    levels_of(0)
    pl.semaphore_wait(barrier, DEVICES - 1)
    halo_copy(0).start()

    def rest(quad, carry):
        levels_of(quad)
        halo_copy(quad).start()
        return carry

    lax.fori_loop(1, QUADS, rest, 0)

    slots = iota((1, OBS), 1)
    for b in range(BLOCKS):
        live = slots < cnt_ref[b : b + 1, :]
        square = jnp.where(live, 1.0 / (err_ref[b : b + 1, :] * (MEMBERS - 1.0)), 0.0)
        valued = square * val_ref[b : b + 1, :]
        easting = east_ref[b : b + 1, :]
        column = TILE_WIDTH * b - HC + col_ref[b : b + 1, :]
        at_slab = iota((SLABS, OBS), 0) == (easting // PLANES)
        left_side = jnp.concatenate(
            [jnp.where(at_slab, square, 0.0), jnp.where(at_slab, valued, 0.0)], axis=0
        )
        high, low = halves(left_side)
        both = jnp.concatenate([high, low], axis=0)
        cell = iota((CELLS, OBS), 0)
        base = (easting % PLANES) * OWN

        def spread(inside, offset):
            at = jnp.where(inside, base + column + offset, -1)
            hot = jnp.where(cell == at, 1.0, 0.0).astype(jnp.bfloat16)
            got = nt(both, hot)
            return got[: 2 * SLABS] + got[2 * SLABS :]

        maps[b] = spread((column >= 0) & (column < OWN), 0)
        if b == 0:
            edge_out[0] = spread(column < 0, OWN)
        if b == BLOCKS - 1:
            edge_out[1] = spread(column >= OWN, -OWN)

    def edge_copy(side):
        return pltpu.make_async_remote_copy(
            src_ref=edge_out.at[side],
            dst_ref=edge_in.at[side],
            send_sem=edge_send.at[side],
            recv_sem=edge_recv.at[side],
            device_id=(left, right)[side],
            device_id_type=MESH,
        )

    edge_copy(0).start()
    edge_copy(1).start()

    spot = iota((LANES, LANES), 0)
    across = iota((LANES, LANES), 1)

    def member(r):
        return 24 * (r // 24) + 12 * ((r // 4) % 2) + 4 * ((r // 8) % 3) + r % 4

    one = jnp.float32(1.0)
    zero = jnp.float32(0.0)
    hot = jnp.where(asg_ref[...] == across, one, zero).astype(jnp.bfloat16)
    order = jnp.where((member(spot) == across) & (spot < MEMBERS), one, zero).astype(jnp.bfloat16)
    slot_rows = nn(order, hot).astype(jnp.bfloat16)
    select[...] = nt(order, slot_rows).astype(jnp.bfloat16)

    def forecast(quad, carry):
        halo_copy(quad).wait_recv()
        for level in range(STEPS):
            read = source(quad, level)

            def one_tile(tile, carried, level=level, read=read):
                u = read(tile)
                upwind = jnp.stack(
                    [
                        jnp.broadcast_to(
                            halo_in[quad, tile, 6 * i + level : 6 * i + level + 1], (8, LANES)
                        )
                        for i in range(4)
                    ]
                )
                above = jnp.where(first_row, upwind, pltpu.roll(u, 1, 1))
                new, turned = advance(u, above, carried, tile)
                if level < STEPS - 1:
                    state[(level + 1) % 2, tile] = new
                else:
                    flat_row = row[0]
                    flat_lane = lane[0]
                    tiles = swap_rows([new[i] for i in range(4)], flat_row)
                    tiles = swap_lanes(tiles, flat_lane)
                    for q in range(4):
                        outgoing[4 * tile + q, quad] = tiles[q]
                return turned

            lax.fori_loop(0, TILES, one_tile, pltpu.roll(read(TILES - 1), 64, 2), unroll=4)
        return carry

    lax.fori_loop(0, QUADS, forecast, 0)

    def message(buffer, to):
        return buffer.at[to[0] * SLABS + to[1]]

    def each_peer(body):
        def at_slab(i, carry):
            def at_group(j, carry):
                peer_g = (g + j) % GROUPS
                peer_s = (s + i) % SLABS

                @pl.when(i * GROUPS + j > 0)
                def _():
                    body(peer_g, peer_s)

                return carry

            return lax.fori_loop(0, GROUPS, at_group, carry)

        lax.fori_loop(0, SLABS, at_slab, 0)

    def send(peer_g, peer_s):
        pltpu.make_async_remote_copy(
            src_ref=message(outgoing, (peer_g, peer_s)),
            dst_ref=incoming.at[s * GROUPS + g],
            send_sem=send_sem,
            recv_sem=recv_sem.at[s],
            device_id=(peer_g, peer_s),
            device_id_type=MESH,
        ).start()

    each_peer(send)
    incoming[s * GROUPS + g] = outgoing[me]

    edge_copy(0).wait_recv()
    edge_copy(1).wait_recv()
    maps[BLOCKS] = edge_in[1]
    maps[BLOCKS + 1] = edge_in[0]
    acc[...] = jnp.zeros(acc.shape, jnp.float32)

    half_row = iota((12, 8, LANES), 1) < 4
    pad = jnp.zeros((LANES - MEMBERS, CELLS), jnp.bfloat16)

    def gather(i, carry):
        from_slab = (s + SLABS - i) % SLABS

        @pl.when(i == 0)
        def _():
            seven = incoming.at[pl.ds(0, GROUPS - 1)]
            pltpu.make_async_copy(seven, seven, recv_sem.at[from_slab]).wait()

        @pl.when(i > 0)
        def _():
            eight = incoming.at[pl.ds(0, GROUPS)]
            pltpu.make_async_copy(eight, eight, recv_sem.at[from_slab]).wait()

        got = incoming[pl.ds(GROUPS * from_slab, GROUPS)].reshape(4, 2, QUADS, 8, LANES)
        a = got[:, 0].reshape(12, 8, LANES)
        b = got[:, 1].reshape(12, 8, LANES)
        near = jnp.where(half_row, a, pltpu.roll(b, 4, 1)).reshape(MEMBERS, LANES)
        far = jnp.where(half_row, pltpu.roll(a, 4, 1), b).reshape(MEMBERS, LANES)
        field = jnp.concatenate([near, far], axis=1)
        mean = jnp.sum(field, axis=0, keepdims=True) * (1.0 / MEMBERS)
        mean_of[from_slab] = mean
        away = field - mean
        high, low = halves(away)
        right_side = jnp.concatenate([high, pad, low, pad], axis=0)
        split[from_slab] = right_side
        pieces = []
        for b in range(BLOCKS + 2):
            omega = maps[b, pl.ds(from_slab, 1)]
            v = maps[b, pl.ds(SLABS + from_slab, 1)]
            pieces.append(omega * away)
            pieces.append(jnp.broadcast_to(v - mean * omega, (ROWS - MEMBERS, CELLS)))
        lhs_high, lhs_low = halves(jnp.concatenate(pieces, axis=0))
        high_part = nt(lhs_high, right_side)
        low_part = nt(lhs_low, right_side[:LANES])
        total = high_part[:, :LANES] + high_part[:, LANES:] + low_part
        acc[...] += total.reshape(acc.shape)
        return carry

    lax.fori_loop(0, SLABS, gather, 0)

    def part_copy(side):
        return pltpu.make_async_remote_copy(
            src_ref=acc.at[BLOCKS + side],
            dst_ref=part_in.at[side],
            send_sem=part_send.at[side],
            recv_sem=part_recv.at[side],
            device_id=(left, right)[side],
            device_id_type=MESH,
        )

    part_copy(0).start()
    part_copy(1).start()

    identity = jnp.where((spot == across) & (spot < MEMBERS), one, zero)
    empty = jnp.zeros((LANES - MEMBERS, LANES), jnp.float32)
    part_copy(0).wait_recv()
    part_copy(1).wait_recv()
    totals = [acc[b] for b in range(BLOCKS)]
    totals[BLOCKS - 1] = totals[BLOCKS - 1] + part_in[0]
    totals[0] = totals[0] + part_in[1]
    grams = [identity + jnp.concatenate([t[:MEMBERS], empty], axis=0) for t in totals]
    fros = [jnp.sqrt(jnp.sum(t * t, keepdims=True)) for t in grams]
    a_of = [t / f for t, f in zip(grams, fros)]
    middles = [1.5 * identity - 0.5 * a for a in a_of]
    z_of = middles
    a_of = [product(a, r) for a, r in zip(a_of, middles)]
    for iteration in range(1, ITERS):
        middles = [1.5 * identity - 0.5 * product(z, a) for z, a in zip(z_of, a_of)]
        if iteration < ITERS - 1:
            a_of = [product(a, r) for a, r in zip(a_of, middles)]
        z_of = [product(r, z) for r, z in zip(middles, z_of)]
    for b in range(BLOCKS):
        transform = z_of[b] * (1.0 / jnp.sqrt(fros[b]))
        projected = jnp.broadcast_to(totals[b][MEMBERS : MEMBERS + 1], (16, LANES))
        mean_weights = product(product(projected, transform), transform)[:1]
        high, low = halves(transform)
        both = nn(select[...], jnp.concatenate([high, low], axis=1))
        by_member = (both[:MEMBERS, :LANES] + both[:MEMBERS, LANES:]) + mean_weights
        high, low = halves(by_member)
        ordered[0, MEMBERS * b : MEMBERS * (b + 1)] = jnp.concatenate([high, high], axis=1)
        ordered[1, MEMBERS * b : MEMBERS * (b + 1)] = jnp.concatenate([low, low], axis=1)

    all_but_one = outgoing.at[pl.ds(0, DEVICES - 1)]
    pltpu.make_async_copy(all_but_one, all_but_one, send_sem).wait()

    block_of = (iota((MEMBERS, CELLS), 1) % OWN) // TILE_WIDTH

    def give_back(i, carry):
        to_slab = (s + i) % SLABS
        right_side = split[to_slab]
        parts = nn(ordered[0], right_side) + nn(ordered[1], right_side)
        field = parts[:MEMBERS]
        for b in range(1, BLOCKS):
            field = jnp.where(block_of == b, parts[MEMBERS * b : MEMBERS * (b + 1)], field)
        field = field + mean_of[to_slab]
        near = field[:, :LANES].reshape(12, 8, LANES)
        far = field[:, LANES:].reshape(12, 8, LANES)
        even = jnp.where(half_row, near, pltpu.roll(far, 4, 1)).reshape(4, QUADS, 8, LANES)
        odd = jnp.where(half_row, pltpu.roll(near, 4, 1), far).reshape(4, QUADS, 8, LANES)
        for a in range(4):
            incoming[GROUPS * to_slab + 2 * a] = even[a]
            incoming[GROUPS * to_slab + 2 * a + 1] = odd[a]

        def to_group(j, carry):
            peer_g = (g + j) % GROUPS

            @pl.when(i * GROUPS + j > 0)
            def _():
                pltpu.make_async_remote_copy(
                    src_ref=incoming.at[GROUPS * to_slab + peer_g],
                    dst_ref=returned.at[me],
                    send_sem=back_send,
                    recv_sem=back_recv,
                    device_id=(peer_g, to_slab),
                    device_id_type=MESH,
                ).start()

            return carry

        lax.fori_loop(0, GROUPS, to_group, 0)
        return carry

    lax.fori_loop(0, SLABS, give_back, 0)
    returned[me] = incoming[s * GROUPS + g]

    for quad in range(QUADS):
        halo_copy(quad).wait_send()
    for side in range(2):
        edge_copy(side).wait_send()
        part_copy(side).wait_send()
    sent = incoming.at[pl.ds(0, DEVICES - 1)]
    pltpu.make_async_copy(sent, sent, back_send).wait()
    got = returned.at[pl.ds(0, DEVICES - 1)]
    pltpu.make_async_copy(got, got, back_recv).wait()

    def unpack(tile, carry):
        for quad in range(QUADS):
            tiles = swap_lanes([returned[4 * tile + q, quad] for q in range(4)], lane[0])
            tiles = swap_rows(tiles, row[0])
            for i in range(4):
                o_ref[4 * quad + i, tile] = tiles[i]
        return carry

    lax.fori_loop(0, TILES, unpack, 0, unroll=2)


def shards(
    initial_samples,
    transport_ratios,
    assignment,
    obs_values,
    obs_error,
    sensor_easting_offset,
    obs_column,
    obs_count,
):
    members, planes, columns = initial_samples.shape

    def tiled(x):
        return jnp.transpose(x.reshape(-1, planes, TILES, LANES), (0, 2, 1, 3))

    f32 = jnp.float32
    bf16 = jnp.bfloat16
    dma = pltpu.SemaphoreType.DMA
    vmem = pl.BlockSpec(memory_space=pltpu.VMEM)
    slot_member = jnp.pad(assignment, (0, LANES - MEMBERS), constant_values=-1)[:, None]
    out = pl.pallas_call(
        kernel,
        name="analysis",
        out_shape=jax.ShapeDtypeStruct((members, TILES, planes, LANES), f32),
        in_specs=[vmem] * 8,
        out_specs=vmem,
        scratch_shapes=[
            pltpu.VMEM((2, TILES, 4, 8, LANES), f32),
            pltpu.VMEM((QUADS, TILES, 24, LANES), f32),
            pltpu.VMEM((QUADS, TILES, 24, LANES), f32),
            pltpu.VMEM((DEVICES, QUADS, 8, LANES), f32),
            pltpu.VMEM((DEVICES, QUADS, 8, LANES), f32),
            pltpu.VMEM((DEVICES, QUADS, 8, LANES), f32),
            pltpu.VMEM((SLABS, 2 * LANES, CELLS), bf16),
            pltpu.VMEM((SLABS, 1, CELLS), f32),
            pltpu.VMEM((BLOCKS + 2, 2 * SLABS, CELLS), f32),
            pltpu.VMEM((2, 2 * SLABS, CELLS), f32),
            pltpu.VMEM((2, 2 * SLABS, CELLS), f32),
            pltpu.VMEM((BLOCKS + 2, ROWS, LANES), f32),
            pltpu.VMEM((2, ROWS, LANES), f32),
            pltpu.VMEM((LANES, LANES), bf16),
            pltpu.VMEM((2, BLOCKS * MEMBERS, 2 * LANES), bf16),
            dma((QUADS,)),
            dma((QUADS,)),
            dma((2,)),
            dma((2,)),
            dma((2,)),
            dma((2,)),
            dma,
            dma((SLABS,)),
            dma,
            dma,
        ],
        compiler_params=pltpu.CompilerParams(
            collective_id=0, has_side_effects=True, vmem_limit_bytes=48 << 20
        ),
    )(
        tiled(initial_samples),
        tiled(transport_ratios),
        slot_member,
        obs_values,
        obs_error,
        sensor_easting_offset,
        obs_column,
        obs_count[:, None],
    )
    return jnp.transpose(out, (0, 2, 1, 3)).reshape(members, planes, columns)


def solution(mesh):
    placed = (
        P("group", "slab", None),
        P(None, "slab", None),
        P(),
        P(("group", "slab"), None),
        P(("group", "slab"), None),
        P(("group", "slab"), None),
        P(("group", "slab"), None),
        P(("group", "slab")),
    )
    return jax.shard_map(
        shards, mesh=mesh, in_specs=placed, out_specs=P("group", "slab", None), check_vma=False
    )
```

time: 259 us -> 126 us (0.49); the launches traced: 255 us -> 125 us
  Pallas kernels: 0 us -> 117 us
  local copies, waits for them, and re-layouts: 88.9 us -> 7.84 us
  waiting for transfers between devices: 61.8 us -> 0 us
  other arithmetic: 32.5 us -> 0 us
  blocking collectives: 31.1 us -> 0 us
  starting transfers between devices: 20.8 us -> 0 us
  matrix products: 18.5 us -> 0 us
    pallas_call x0 -> x1, Pallas kernels: none -> 117 us  [shards(): pl.pallas_call(kernel, name='analysis', out_shape=jax.ShapeDtypeStruct((m...]
    ppermute x6 -> x0, waiting for transfers between devices: 38.1 us -> none  [the longest x2 38 us: shifted(): return lax.ppermute(block, axis, route)]
    all_to_all x1 -> x0, blocking collectives: 31.1 us -> none  [joined_exchange(): lax.all_to_all(pieces, axis, split_axis=0, concat_axis=0, tiled=True)]
    all_to_all x1 -> x0, waiting for transfers between devices: 23.7 us -> none  [joined_exchange(): lax.all_to_all(pieces, axis, split_axis=0, concat_axis=0, tiled=True)]
    another operation x3 -> x0, local copies, waits for them, and re-layouts: 19.6 us -> none  [the longest x2 13.5 us: joined_exchange(): pieces = jnp.moveaxis(split_up(pieces, splits[1] + 1, sizes[1]), 0, 1)]
    transpose x3 -> x0, local copies, waits for them, and re-layouts: 19.6 us -> none  [joined_along(): return jnp.moveaxis(pieces, 0, dim).reshape(shape)]
    dot_general x29 -> x0, matrix products: 18.5 us -> none  [the longest x1 5.48 us: shards(): jnp.einsum('cmj,cmx->cjx', column_weights, column_major - cell_mean[:, No...]
    sub x8 -> x0, other arithmetic: 18.5 us -> none  [the longest x6 17.9 us: advance(): sample_state - rates[0] * (sample_state - upwind)]
  transfers between devices with their start and end apart: 7 -> 0, of which waited for: 3 -> 0; matrix products, arithmetic and copies ran while one was open for 22% -> 0% of each run, Pallas kernels for 0% -> 0%
where the time goes in v1:
time: 126 us; the launch traced here: 125 us
  Pallas kernels  117 us (93%)
  local copies, waits for them, and re-layouts  7.84 us (6%)
    pallas_call x1, Pallas kernels, shards(): pl.pallas_call(kernel, name='analysis', out_shape=jax.ShapeDtypeStruct((m...  117 us
    unnamed x13, local copies, waits for them, and re-layouts  6.33 us

profile of v1, /device:TPU:1, one launch (start us, length us, event | category | flops | bytes accessed | tf_op | source)
XLA Modules:
  0.0 124.7 jit_solution(7293580937175754244)
XLA Ops:
  0.0 0.7 pad_bitcast_fusion
  0.7 0.7 copy.10.cnt_ref
  1.4 0.1 copy.9.asg_ref
  1.5 0.0 copy-start
  1.5 1.4 %copy-done = f32[12,8,4096]{2,1,0:T(8,128)S(1)} copy-done((f32[12,8,4096]{2,1,0:T(8,128)S(1)}, f32[12,8,4096]{2,1,0:T(8,128)}, u32[]{:S(2)}) %copy-start) | copy-done | bytes 1572888
  2.9 0.0 copy-start.1
  2.9 1.0 copy-done.1
  3.9 0.0 copy-start.2
  3.9 0.7 copy-done.2
  4.6 0.0 copy-start.3
  4.6 0.7 copy-done.3
  5.3 0.0 copy-start.4
  5.3 0.7 copy-done.4
  6.0 0.0 copy-start.5
  6.0 0.7 copy-done.5
  6.7 116.8 %analysis.1 = f32[12,32,8,128]{3,2,1,0:T(8,128)S(1)} custom-call(f32[12,32,8,128]{3,2,1,0:T(8,128)S(1)} %bitcast.13, f32[3,32,8,128]{3,2,1,0:T(8,128)S(1)} %bitcast.14, s32[128,1]{1,0:T(8,128)S(1)} %copy.9.asg_ref, f32[4,512]{1,0:T(4,128)S(1)} %copy-done.2, f32[4,512]{1,0:T(4,128)S(1)} %copy-done.3, s32[4,512]{1,0:T(4,128)S(1)} %copy-done.4, ...), custom_call_target="tpu_custom_call" | custom-call | tf_op jit(solution)/shard_map/analysis/pallas_call | solution.py:502
  123.5 1.1 copy.12
Async XLA Ops:
  1.5 1.4 %copy-start = (f32[12,8,4096]{2,1,0:T(8,128)S(1)}, f32[12,8,4096]{2,1,0:T(8,128)}, u32[]{:S(2)}) copy-start(f32[12,8,4096]{2,1,0:T(8,128)} %param.8) | copy-start | bytes 4718596
  2.9 1.0 copy-start.1
  3.9 0.7 copy-start.2
  4.6 0.7 copy-start.3
  5.3 0.7 copy-start.4
  6.0 0.7 copy-start.5

commit v2 on v1

--- a/solution.py
+++ b/solution.py
@@ -24,7 +24,7 @@
 BLOCKS = 4
 CELLS = PLANES * OWN
 ROWS = 112
-MESH = pl.DeviceIdType.MESH
+LOGICAL = pl.DeviceIdType.LOGICAL
 
 
 def nt(a, b):
@@ -84,7 +84,29 @@
     return lax.broadcasted_iota(jnp.int32, shape, dim)
 
 
+def transposed(tiles, row):
+    axis = tiles[0].ndim - 2
+    tiles = list(tiles)
+    for d in (4, 2, 1):
+        upper = (row & d) == 0
+        for j in range(8):
+            if not j & d:
+                a, b = tiles[j], tiles[j + d]
+                tiles[j] = jnp.where(upper, a, pltpu.roll(b, d, axis))
+                tiles[j + d] = jnp.where(upper, pltpu.roll(a, 8 - d, axis), b)
+    return tiles
+
+
 def kernel(
+    x_hbm,
+    c_hbm,
+    asg_hbm,
+    val_hbm,
+    err_hbm,
+    east_hbm,
+    col_hbm,
+    cnt_hbm,
+    o_ref,
     x_ref,
     c_ref,
     asg_ref,
@@ -93,10 +115,8 @@
     east_ref,
     col_ref,
     cnt_ref,
-    o_ref,
+    rates,
     state,
-    halo_out,
-    halo_in,
     outgoing,
     incoming,
     returned,
@@ -109,6 +129,8 @@
     part_in,
     select,
     ordered,
+    x_sem,
+    small_sem,
     halo_send,
     halo_recv,
     edge_send,
@@ -123,103 +145,156 @@
     g = lax.axis_index("group")
     s = lax.axis_index("slab")
     me = g * SLABS + s
-
-    def place(d):
-        return (d // SLABS, d % SLABS)
-
-    left = place((me + DEVICES - 1) % DEVICES)
-    right = place((me + 1) % DEVICES)
+    left = (me + DEVICES - 1) % DEVICES
+    right = (me + 1) % DEVICES
+
+    rate_copy = pltpu.make_async_copy(c_hbm, c_ref, small_sem.at[0])
+    rate_copy.start()
+
+    def sample_copy(quad):
+        four = pl.ds(4 * quad, 4)
+        return pltpu.make_async_copy(x_hbm.at[four], x_ref.at[four], x_sem.at[quad])
+
+    for quad in range(QUADS):
+        sample_copy(quad).start()
+    small_copies = [
+        pltpu.make_async_copy(source, target, small_sem.at[1 + i])
+        for i, (source, target) in enumerate(
+            [
+                (asg_hbm, asg_ref),
+                (val_hbm, val_ref),
+                (err_hbm, err_ref),
+                (east_hbm, east_ref),
+                (col_hbm, col_ref),
+                (cnt_hbm, cnt_ref),
+            ]
+        )
+    ]
+    for copy in small_copies:
+        copy.start()
 
     barrier = pltpu.get_barrier_semaphore()
 
     def greet(i, carry):
         pl.semaphore_signal(
-            barrier, inc=1, device_id=place((me + i) % DEVICES), device_id_type=MESH
+            barrier, inc=1, device_id=(me + i) & (DEVICES - 1), device_id_type=LOGICAL
         )
         return carry
 
-    lax.fori_loop(1, DEVICES, greet, 0)
-
-    row = iota((4, 8, LANES), 1)
-    lane = iota((4, 8, LANES), 2)
-    first_row = row == 0
+    lax.fori_loop(1, DEVICES, greet, 0, unroll=8)
+
+    row = iota((8, LANES), 0)
+    lane = iota((8, LANES), 1)
+    upper_half = row < 4
     low_half = lane < 64
     z_first = (lane & (NZ - 1)) == 0
 
-    def advance(u, above, carried, tile):
-        turned = pltpu.roll(u, 64, 2)
-        below_y = jnp.where(low_half, carried, turned)
-        below_z = jnp.where(z_first, pltpu.roll(turned, 1, 2), pltpu.roll(u, 1, 2))
-        new = (
+    def lanes_swapped(a, b):
+        first = jnp.where(low_half, a, pltpu.roll(b, 64, 1))
+        second = jnp.where(low_half, pltpu.roll(a, 64, 1), b)
+        return jnp.stack([first, second])
+
+    rate_copy.wait()
+
+    def take_rates(u, carry):
+        for i in range(3):
+            sides = [
+                lanes_swapped(c_ref[i, u + 16 * h], c_ref[i, u + 16 * h + 8]) for h in range(2)
+            ]
+            for x in range(PLANES):
+                rates[i, x, pl.ds(2 * u, 2)] = jnp.where(
+                    upper_half, sides[0][:, x : x + 1], sides[1][:, x : x + 1]
+                )
+        return carry
+
+    lax.fori_loop(0, 8, take_rates, 0)
+
+    def wrap(quad, level, first, end):
+        last = state[quad, level, first + 1 : end + 1, 16]
+        turned = pltpu.roll(last, 64, 2)
+        state[quad, level, first + 1 : end + 1, 0] = jnp.where(
+            low_half, pltpu.roll(turned, 4, 1), turned
+        )
+
+    def take_samples(quad):
+        sample_copy(quad).wait()
+
+        def one(u, carry):
+            tiles = []
+            for h in range(2):
+                for i in range(4):
+                    at = 4 * quad + i
+                    tiles.append(lanes_swapped(x_ref[at, u + 16 * h], x_ref[at, u + 16 * h + 8]))
+            for x, tile in enumerate(transposed(tiles, row)):
+                state[quad, 0, x + 1, pl.ds(2 * u + 1, 2)] = tile
+            return carry
+
+        lax.fori_loop(0, 8, one, 0)
+        wrap(quad, 0, 0, PLANES)
+
+    def stepped(quad, level, first, end, ty):
+        u = state[quad, level, first + 1 : end + 1, ty + 1]
+        above = state[quad, level, first:end, ty + 1]
+        below_y = state[quad, level, first + 1 : end + 1, ty]
+        below_z = jnp.where(z_first, pltpu.roll(u, 65, 2), pltpu.roll(u, 1, 2))
+        return (
             u
-            - c_ref[0, tile] * (u - above)
-            - c_ref[1, tile] * (u - below_y)
-            - c_ref[2, tile] * (u - below_z)
-        )
-        return new, turned
-
-    def source(quad, level):
-        if level == 0:
-            return lambda tile: x_ref[pl.ds(4 * quad, 4), tile]
-        return lambda tile: state[level % 2, tile]
-
-    def levels_of(quad):
+            - rates[0, first:end, ty] * (u - above)
+            - rates[1, first:end, ty] * (u - below_y)
+            - rates[2, first:end, ty] * (u - below_z)
+        )
+
+    def advance(quad, level, first, end):
+        def one(ty, carry):
+            new = stepped(quad, level, first, end, ty)
+            state[quad, level + 1, first + 1 : end + 1, ty + 1] = new
+            return carry
+
+        lax.fori_loop(0, 16, one, 0, unroll=2)
+        wrap(quad, level + 1, first, end)
+
+    def own_cone(quad):
+        take_samples(quad)
         for level in range(STEPS - 1):
-            read = source(quad, level)
-
-            def one(tile, carried, level=level, read=read):
-                u = read(tile)
-                if level == 0:
-                    for i in range(4):
-                        halo_out[quad, tile, 6 * i : 6 * i + 1] = u[i, 7:8]
-                new, turned = advance(u, pltpu.roll(u, 1, 1), carried, tile)
-                if level < STEPS - 2:
-                    state[(level + 1) % 2, tile] = new
-                for i in range(4):
-                    at = 6 * i + level + 1
-                    halo_out[quad, tile, at : at + 1] = new[i, 7:8]
-                return turned
-
-            lax.fori_loop(0, TILES, one, pltpu.roll(read(TILES - 1), 64, 2), unroll=4)
-
-    next_slab = (g, (s + 1) % SLABS)
+            advance(quad, level, level + 3, PLANES)
+
+    next_slab = g * SLABS + (s + 1) % SLABS
 
     def halo_copy(quad):
         return pltpu.make_async_remote_copy(
-            src_ref=halo_out.at[quad],
-            dst_ref=halo_in.at[quad],
+            src_ref=state.at[quad, :, PLANES, pl.ds(1, 16)],
+            dst_ref=state.at[quad, :, 0, pl.ds(1, 16)],
             send_sem=halo_send.at[quad],
             recv_sem=halo_recv.at[quad],
             device_id=next_slab,
-            device_id_type=MESH,
-        )
-
-    levels_of(0)
+            device_id_type=LOGICAL,
+        )
+
+    own_cone(0)
     pl.semaphore_wait(barrier, DEVICES - 1)
     halo_copy(0).start()
-
-    def rest(quad, carry):
-        levels_of(quad)
-        halo_copy(quad).start()
-        return carry
-
-    lax.fori_loop(1, QUADS, rest, 0)
+    own_cone(1)
+    halo_copy(1).start()
+    own_cone(2)
+
+    for copy in small_copies:
+        copy.wait()
 
     slots = iota((1, OBS), 1)
     for b in range(BLOCKS):
-        live = slots < cnt_ref[b : b + 1, :]
+        live = slots < cnt_ref[:, b : b + 1]
         square = jnp.where(live, 1.0 / (err_ref[b : b + 1, :] * (MEMBERS - 1.0)), 0.0)
         valued = square * val_ref[b : b + 1, :]
         easting = east_ref[b : b + 1, :]
         column = TILE_WIDTH * b - HC + col_ref[b : b + 1, :]
-        at_slab = iota((SLABS, OBS), 0) == (easting // PLANES)
+        at_slab = iota((SLABS, OBS), 0) == (easting >> 3)
         left_side = jnp.concatenate(
             [jnp.where(at_slab, square, 0.0), jnp.where(at_slab, valued, 0.0)], axis=0
         )
         high, low = halves(left_side)
         both = jnp.concatenate([high, low], axis=0)
         cell = iota((CELLS, OBS), 0)
-        base = (easting % PLANES) * OWN
+        base = (easting & (PLANES - 1)) * OWN
 
         def spread(inside, offset):
             at = jnp.where(inside, base + column + offset, -1)
@@ -240,7 +315,7 @@
             send_sem=edge_send.at[side],
             recv_sem=edge_recv.at[side],
             device_id=(left, right)[side],
-            device_id_type=MESH,
+            device_id_type=LOGICAL,
         )
 
     edge_copy(0).start()
@@ -254,71 +329,56 @@
 
     one = jnp.float32(1.0)
     zero = jnp.float32(0.0)
-    hot = jnp.where(asg_ref[...] == across, one, zero).astype(jnp.bfloat16)
+    slot_lane = iota((LANES, MEMBERS), 1)
+    slot_spot = iota((LANES, MEMBERS), 0)
+    hot = jnp.where(asg_ref[...] == slot_spot, one, zero).astype(jnp.bfloat16)
     order = jnp.where((member(spot) == across) & (spot < MEMBERS), one, zero).astype(jnp.bfloat16)
-    slot_rows = nn(order, hot).astype(jnp.bfloat16)
-    select[...] = nt(order, slot_rows).astype(jnp.bfloat16)
-
-    def forecast(quad, carry):
+    slot_order = jnp.where((member(slot_spot) == slot_lane) & (slot_spot < MEMBERS), one, zero)
+    member_rows = nn(order, hot).astype(jnp.bfloat16)
+    select[...] = nt(member_rows, slot_order.astype(jnp.bfloat16)).astype(jnp.bfloat16)
+
+    def forecast(quad):
         halo_copy(quad).wait_recv()
-        for level in range(STEPS):
-            read = source(quad, level)
-
-            def one_tile(tile, carried, level=level, read=read):
-                u = read(tile)
-                upwind = jnp.stack(
-                    [
-                        jnp.broadcast_to(
-                            halo_in[quad, tile, 6 * i + level : 6 * i + level + 1], (8, LANES)
-                        )
-                        for i in range(4)
-                    ]
-                )
-                above = jnp.where(first_row, upwind, pltpu.roll(u, 1, 1))
-                new, turned = advance(u, above, carried, tile)
-                if level < STEPS - 1:
-                    state[(level + 1) % 2, tile] = new
-                else:
-                    flat_row = row[0]
-                    flat_lane = lane[0]
-                    tiles = swap_rows([new[i] for i in range(4)], flat_row)
-                    tiles = swap_lanes(tiles, flat_lane)
-                    for q in range(4):
-                        outgoing[4 * tile + q, quad] = tiles[q]
-                return turned
-
-            lax.fori_loop(0, TILES, one_tile, pltpu.roll(read(TILES - 1), 64, 2), unroll=4)
-        return carry
-
-    lax.fori_loop(0, QUADS, forecast, 0)
-
-    def message(buffer, to):
-        return buffer.at[to[0] * SLABS + to[1]]
+        for level in range(STEPS - 1):
+            advance(quad, level, 0, level + 3)
+
+        def pack(ty, carry):
+            new = stepped(quad, STEPS - 1, 0, PLANES, ty)
+            for h in range(2):
+                tiles = []
+                for x in range(4):
+                    a, b = new[x], new[4 + x]
+                    if h == 0:
+                        tiles.append(jnp.where(upper_half, a, pltpu.roll(b, 4, 0)))
+                    else:
+                        tiles.append(jnp.where(upper_half, pltpu.roll(a, 4, 0), b))
+                for i, tile in enumerate(swap_lanes(tiles, lane)):
+                    outgoing[64 * h + 32 * (i // 2) + 2 * ty + i % 2, quad] = tile
+            return carry
+
+        lax.fori_loop(0, 16, pack, 0)
+
+    halo_copy(0).wait_send()
+    halo_copy(2).start()
+    for quad in range(QUADS):
+        forecast(quad)
 
     def each_peer(body):
-        def at_slab(i, carry):
-            def at_group(j, carry):
-                peer_g = (g + j) % GROUPS
-                peer_s = (s + i) % SLABS
-
-                @pl.when(i * GROUPS + j > 0)
-                def _():
-                    body(peer_g, peer_s)
-
-                return carry
-
-            return lax.fori_loop(0, GROUPS, at_group, carry)
-
-        lax.fori_loop(0, SLABS, at_slab, 0)
+        def one(k, carry):
+            body((g + (k >> 4)) & (GROUPS - 1), (s + k) & (SLABS - 1))
+            return carry
+
+        lax.fori_loop(1, DEVICES, one, 0, unroll=2)
 
     def send(peer_g, peer_s):
+        peer = peer_g * SLABS + peer_s
         pltpu.make_async_remote_copy(
-            src_ref=message(outgoing, (peer_g, peer_s)),
+            src_ref=outgoing.at[peer],
             dst_ref=incoming.at[s * GROUPS + g],
             send_sem=send_sem,
             recv_sem=recv_sem.at[s],
-            device_id=(peer_g, peer_s),
-            device_id_type=MESH,
+            device_id=peer,
+            device_id_type=LOGICAL,
         ).start()
 
     each_peer(send)
@@ -380,7 +440,7 @@
             send_sem=part_send.at[side],
             recv_sem=part_recv.at[side],
             device_id=(left, right)[side],
-            device_id_type=MESH,
+            device_id_type=LOGICAL,
         )
 
     part_copy(0).start()
@@ -437,7 +497,7 @@
             incoming[GROUPS * to_slab + 2 * a + 1] = odd[a]
 
         def to_group(j, carry):
-            peer_g = (g + j) % GROUPS
+            peer_g = (g + j) & (GROUPS - 1)
 
             @pl.when(i * GROUPS + j > 0)
             def _():
@@ -446,8 +506,8 @@
                     dst_ref=returned.at[me],
                     send_sem=back_send,
                     recv_sem=back_recv,
-                    device_id=(peer_g, to_slab),
-                    device_id_type=MESH,
+                    device_id=peer_g * SLABS + to_slab,
+                    device_id_type=LOGICAL,
                 ).start()
 
             return carry
@@ -458,8 +518,8 @@
     lax.fori_loop(0, SLABS, give_back, 0)
     returned[me] = incoming[s * GROUPS + g]
 
-    for quad in range(QUADS):
-        halo_copy(quad).wait_send()
+    halo_copy(1).wait_send()
+    halo_copy(2).wait_send()
     for side in range(2):
         edge_copy(side).wait_send()
         part_copy(side).wait_send()
@@ -470,8 +530,8 @@
 
     def unpack(tile, carry):
         for quad in range(QUADS):
-            tiles = swap_lanes([returned[4 * tile + q, quad] for q in range(4)], lane[0])
-            tiles = swap_rows(tiles, row[0])
+            tiles = swap_lanes([returned[4 * tile + q, quad] for q in range(4)], lane)
+            tiles = swap_rows(tiles, row)
             for i in range(4):
                 o_ref[4 * quad + i, tile] = tiles[i]
         return carry
@@ -495,20 +555,27 @@
         return jnp.transpose(x.reshape(-1, planes, TILES, LANES), (0, 2, 1, 3))
 
     f32 = jnp.float32
+    i32 = jnp.int32
     bf16 = jnp.bfloat16
     dma = pltpu.SemaphoreType.DMA
-    vmem = pl.BlockSpec(memory_space=pltpu.VMEM)
-    slot_member = jnp.pad(assignment, (0, LANES - MEMBERS), constant_values=-1)[:, None]
+    hbm = pl.BlockSpec(memory_space=pltpu.HBM)
     out = pl.pallas_call(
         kernel,
         name="analysis",
         out_shape=jax.ShapeDtypeStruct((members, TILES, planes, LANES), f32),
-        in_specs=[vmem] * 8,
-        out_specs=vmem,
+        in_specs=[hbm] * 8,
+        out_specs=pl.BlockSpec(memory_space=pltpu.VMEM),
         scratch_shapes=[
-            pltpu.VMEM((2, TILES, 4, 8, LANES), f32),
-            pltpu.VMEM((QUADS, TILES, 24, LANES), f32),
-            pltpu.VMEM((QUADS, TILES, 24, LANES), f32),
+            pltpu.VMEM((4 * QUADS, TILES, PLANES, LANES), f32),
+            pltpu.VMEM((3, TILES, PLANES, LANES), f32),
+            pltpu.VMEM((1, MEMBERS), i32),
+            pltpu.VMEM((BLOCKS, OBS), f32),
+            pltpu.VMEM((BLOCKS, OBS), f32),
+            pltpu.VMEM((BLOCKS, OBS), i32),
+            pltpu.VMEM((BLOCKS, OBS), i32),
+            pltpu.VMEM((1, BLOCKS), i32),
+            pltpu.VMEM((3, PLANES, 16, 8, LANES), f32),
+            pltpu.VMEM((QUADS, STEPS, PLANES + 1, 17, 8, LANES), f32),
             pltpu.VMEM((DEVICES, QUADS, 8, LANES), f32),
             pltpu.VMEM((DEVICES, QUADS, 8, LANES), f32),
             pltpu.VMEM((DEVICES, QUADS, 8, LANES), f32),
@@ -522,6 +589,8 @@
             pltpu.VMEM((LANES, LANES), bf16),
             pltpu.VMEM((2, BLOCKS * MEMBERS, 2 * LANES), bf16),
             dma((QUADS,)),
+            dma((7,)),
+            dma((QUADS,)),
             dma((QUADS,)),
             dma((2,)),
             dma((2,)),
@@ -533,17 +602,17 @@
             dma,
         ],
         compiler_params=pltpu.CompilerParams(
-            collective_id=0, has_side_effects=True, vmem_limit_bytes=48 << 20
+            collective_id=0, has_side_effects=True, vmem_limit_bytes=56 << 20
         ),
     )(
         tiled(initial_samples),
         tiled(transport_ratios),
-        slot_member,
+        assignment[None, :],
         obs_values,
         obs_error,
         sensor_easting_offset,
         obs_column,
-        obs_count[:, None],
+        obs_count[None, :],
     )
     return jnp.transpose(out, (0, 2, 1, 3)).reshape(members, planes, columns)
 

time: 126 us -> 108 us (0.86); the launches traced: 125 us -> 108 us
  Pallas kernels: 117 us -> 105 us
  local copies, waits for them, and re-layouts: 7.84 us -> 2.65 us
    pallas_call x1, Pallas kernels: 117 us -> 105 us  [shards(): pl.pallas_call(kernel, name='analysis', out_shape=jax.ShapeDtypeStruct((m...]
    unnamed x13 -> x1, local copies, waits for them, and re-layouts: 6.33 us -> 2.65 us
    broadcast_in_dim x3 -> x0, local copies, waits for them, and re-layouts: 1.51 us -> none  [the longest x2 0.77 us: shards(): jnp.pad(assignment, (0, LANES - MEMBERS), constant_values=-1)[:, None]]
where the time goes in v2:
time: 108 us
  Pallas kernels  105 us (97%)
  local copies, waits for them, and re-layouts  2.65 us (2%)
    pallas_call x1, Pallas kernels, shards(): pl.pallas_call(kernel, name='analysis', out_shape=jax.ShapeDtypeStruct((m...  105 us
    unnamed x1, local copies, waits for them, and re-layouts  2.65 us

profile of v2, /device:TPU:1, one launch (start us, length us, event | category | flops | bytes accessed | tf_op | source)
XLA Modules:
  0.0 108.0 jit_solution(15898842821046399732)
XLA Ops:
  0.0 105.3 %analysis.1 = f32[12,32,8,128]{3,2,1,0:T(8,128)} custom-call(f32[12,32,8,128]{3,2,1,0:T(8,128)} %bitcast.12, f32[3,32,8,128]{3,2,1,0:T(8,128)} %bitcast.13, s32[1,96]{1,0:T(1,128)} %bitcast.14, f32[4,512]{1,0:T(4,128)} %val_hbm.1, f32[4,512]{1,0:T(4,128)} %err_hbm.1, s32[4,512]{1,0:T(4,128)} %east_hbm.1, s32[4,512]{1,0:T(4,128)} %col_hbm.1, s32[1,4]{1,0:T(1,128)} %bitcast.15), custom_call_target="tpu_custom_call" | custom-call | tf_op jit(solution)/shard_map/analysis/pallas_call | solution.py:562
  105.3 2.7 %copy.10 = f32[12,8,4096]{2,1,0:T(8,128)} copy(f32[12,8,4096]{2,1,0:T(8,128)} %bitcast.11) | data formatting | bytes 3145728

commit v3 on v2

--- a/solution.py
+++ b/solution.py
@@ -115,8 +115,10 @@
     east_ref,
     col_ref,
     cnt_ref,
+    c_next,
     rates,
     state,
+    ahead,
     outgoing,
     incoming,
     returned,
@@ -196,27 +198,31 @@
 
     rate_copy.wait()
 
-    def take_rates(u, carry):
-        for i in range(3):
-            sides = [
-                lanes_swapped(c_ref[i, u + 16 * h], c_ref[i, u + 16 * h + 8]) for h in range(2)
-            ]
-            for x in range(PLANES):
-                rates[i, x, pl.ds(2 * u, 2)] = jnp.where(
-                    upper_half, sides[0][:, x : x + 1], sides[1][:, x : x + 1]
-                )
-        return carry
-
-    lax.fori_loop(0, 8, take_rates, 0)
-
-    def wrap(quad, level, first, end):
-        last = state[quad, level, first + 1 : end + 1, 16]
+    def take_rates(source, planes, offset):
+        def one(u, carry):
+            for i in range(3):
+                sides = [
+                    lanes_swapped(source[i, u + 16 * h], source[i, u + 16 * h + 8])
+                    for h in range(2)
+                ]
+                for x in range(planes):
+                    rates[i, offset + x, pl.ds(2 * u, 2)] = jnp.where(
+                        upper_half, sides[0][:, x : x + 1], sides[1][:, x : x + 1]
+                    )
+            return carry
+
+        lax.fori_loop(0, 8, one, 0)
+
+    take_rates(c_ref, PLANES, 0)
+
+    def wrap(grid, level, first, end):
+        last = grid[level, first + 1 : end + 1, 16]
         turned = pltpu.roll(last, 64, 2)
-        state[quad, level, first + 1 : end + 1, 0] = jnp.where(
+        grid[level, first + 1 : end + 1, 0] = jnp.where(
             low_half, pltpu.roll(turned, 4, 1), turned
         )
 
-    def take_samples(quad):
+    def take_samples(quad, grid):
         sample_copy(quad).wait()
 
         def one(u, carry):
@@ -226,39 +232,38 @@
                     at = 4 * quad + i
                     tiles.append(lanes_swapped(x_ref[at, u + 16 * h], x_ref[at, u + 16 * h + 8]))
             for x, tile in enumerate(transposed(tiles, row)):
-                state[quad, 0, x + 1, pl.ds(2 * u + 1, 2)] = tile
+                grid[0, x + 1, pl.ds(2 * u + 1, 2)] = tile
             return carry
 
         lax.fori_loop(0, 8, one, 0)
-        wrap(quad, 0, 0, PLANES)
-
-    def stepped(quad, level, first, end, ty):
-        u = state[quad, level, first + 1 : end + 1, ty + 1]
-        above = state[quad, level, first:end, ty + 1]
-        below_y = state[quad, level, first + 1 : end + 1, ty]
-        below_z = jnp.where(z_first, pltpu.roll(u, 65, 2), pltpu.roll(u, 1, 2))
+        wrap(grid, 0, 0, PLANES)
+
+    def stepped(grid, level, first, end, ty, n):
+        u = grid[level, first + 1 : end + 1, pl.ds(ty + 1, n)]
+        above = grid[level, first:end, pl.ds(ty + 1, n)]
+        below_y = grid[level, first + 1 : end + 1, pl.ds(ty, n)]
+        below_z = jnp.where(z_first, pltpu.roll(u, 65, 3), pltpu.roll(u, 1, 3))
         return (
             u
-            - rates[0, first:end, ty] * (u - above)
-            - rates[1, first:end, ty] * (u - below_y)
-            - rates[2, first:end, ty] * (u - below_z)
-        )
-
-    def advance(quad, level, first, end):
-        def one(ty, carry):
-            new = stepped(quad, level, first, end, ty)
-            state[quad, level + 1, first + 1 : end + 1, ty + 1] = new
+            - rates[0, first:end, pl.ds(ty, n)] * (u - above)
+            - rates[1, first:end, pl.ds(ty, n)] * (u - below_y)
+            - rates[2, first:end, pl.ds(ty, n)] * (u - below_z)
+        )
+
+    def advance(grid, level, first, end):
+        planes = end - first
+        n = 16 if planes < 3 else 8 if planes < 6 else 4
+
+        def one(i, carry):
+            new = stepped(grid, level, first, end, n * i, n)
+            grid[level + 1, first + 1 : end + 1, pl.ds(n * i + 1, n)] = new
             return carry
 
-        lax.fori_loop(0, 16, one, 0, unroll=2)
-        wrap(quad, level + 1, first, end)
-
-    def own_cone(quad):
-        take_samples(quad)
-        for level in range(STEPS - 1):
-            advance(quad, level, level + 3, PLANES)
-
-    next_slab = g * SLABS + (s + 1) % SLABS
+        lax.fori_loop(0, 16 // n, one, 0)
+        wrap(grid, level + 1, first, end)
+
+    next_slab = g * SLABS + ((s + 1) & (SLABS - 1))
+    last_slab = g * SLABS + ((s + SLABS - 1) & (SLABS - 1))
 
     def halo_copy(quad):
         return pltpu.make_async_remote_copy(
@@ -270,12 +275,36 @@
             device_id_type=LOGICAL,
         )
 
-    own_cone(0)
+    back_halo = pltpu.make_async_remote_copy(
+        src_ref=ahead.at[0, pl.ds(1, STEPS), pl.ds(1, 16)],
+        dst_ref=ahead.at[0, pl.ds(PLANES + 1, STEPS), pl.ds(1, 16)],
+        send_sem=halo_send.at[2],
+        recv_sem=halo_recv.at[2],
+        device_id=last_slab,
+        device_id_type=LOGICAL,
+    )
+    back_rates = pltpu.make_async_remote_copy(
+        src_ref=c_ref,
+        dst_ref=c_next,
+        send_sem=halo_send.at[3],
+        recv_sem=halo_recv.at[3],
+        device_id=last_slab,
+        device_id_type=LOGICAL,
+    )
+
+    grids = [state.at[0], state.at[1]]
+    for quad in range(2):
+        take_samples(quad, grids[quad])
+        for level in range(STEPS - 1):
+            advance(grids[quad], level, level + 3, PLANES)
+    take_samples(2, ahead)
+
     pl.semaphore_wait(barrier, DEVICES - 1)
     halo_copy(0).start()
-    own_cone(1)
-    halo_copy(1).start()
-    own_cone(2)
+    back_rates.start()
+    back_halo.start()
+    for level in range(STEPS - 1):
+        advance(ahead, level, level + 1, PLANES)
 
     for copy in small_copies:
         copy.wait()
@@ -337,31 +366,44 @@
     member_rows = nn(order, hot).astype(jnp.bfloat16)
     select[...] = nt(member_rows, slot_order.astype(jnp.bfloat16)).astype(jnp.bfloat16)
 
+    def pack_all(quad, grid, first):
+        def pack(i, carry):
+            ty = 4 * i
+            new = stepped(grid, STEPS - 1, first, first + PLANES, ty, 4)
+            at_plane = [new[(x - first) % PLANES] for x in range(PLANES)]
+            for h in range(2):
+                tiles = []
+                for x in range(4):
+                    a, b = at_plane[x], at_plane[4 + x]
+                    if h == 0:
+                        tiles.append(jnp.where(upper_half, a, pltpu.roll(b, 4, 1)))
+                    else:
+                        tiles.append(jnp.where(upper_half, pltpu.roll(a, 4, 1), b))
+                for j, tile in enumerate(swap_lanes(tiles, lane)):
+                    for k in range(4):
+                        at = 64 * h + 32 * (j // 2) + 2 * k + j % 2
+                        outgoing[at + 2 * ty, quad] = tile[k]
+            return carry
+
+        lax.fori_loop(0, 4, pack, 0)
+
     def forecast(quad):
         halo_copy(quad).wait_recv()
         for level in range(STEPS - 1):
-            advance(quad, level, 0, level + 3)
-
-        def pack(ty, carry):
-            new = stepped(quad, STEPS - 1, 0, PLANES, ty)
-            for h in range(2):
-                tiles = []
-                for x in range(4):
-                    a, b = new[x], new[4 + x]
-                    if h == 0:
-                        tiles.append(jnp.where(upper_half, a, pltpu.roll(b, 4, 0)))
-                    else:
-                        tiles.append(jnp.where(upper_half, pltpu.roll(a, 4, 0), b))
-                for i, tile in enumerate(swap_lanes(tiles, lane)):
-                    outgoing[64 * h + 32 * (i // 2) + 2 * ty + i % 2, quad] = tile
-            return carry
-
-        lax.fori_loop(0, 16, pack, 0)
+            advance(grids[quad], level, 0, level + 3)
+        pack_all(quad, grids[quad], 0)
 
     halo_copy(0).wait_send()
-    halo_copy(2).start()
-    for quad in range(QUADS):
-        forecast(quad)
+    halo_copy(1).start()
+    forecast(0)
+    back_rates.wait_recv()
+    take_rates(c_next, STEPS, PLANES)
+    back_halo.wait_recv()
+    wrap(ahead, 0, PLANES, PLANES + STEPS)
+    for level in range(STEPS - 1):
+        advance(ahead, level, PLANES, PLANES + STEPS)
+    pack_all(2, ahead, STEPS)
+    forecast(1)
 
     def each_peer(body):
         def one(k, carry):
@@ -393,20 +435,22 @@
     half_row = iota((12, 8, LANES), 1) < 4
     pad = jnp.zeros((LANES - MEMBERS, CELLS), jnp.bfloat16)
 
+    late = (iota((GROUPS, 8, LANES), 1) >= 4) & (iota((GROUPS, 8, LANES), 2) >= 64)
+    seven = incoming.at[pl.ds(0, GROUPS - 1)]
+    pltpu.make_async_copy(seven, seven, recv_sem.at[s]).wait()
+
     def gather(i, carry):
-        from_slab = (s + SLABS - i) % SLABS
-
-        @pl.when(i == 0)
-        def _():
-            seven = incoming.at[pl.ds(0, GROUPS - 1)]
-            pltpu.make_async_copy(seven, seven, recv_sem.at[from_slab]).wait()
-
-        @pl.when(i > 0)
+        from_slab = (s - i) & (SLABS - 1)
+        before = (s - i - 1) & (SLABS - 1)
+
+        @pl.when(i < SLABS - 1)
         def _():
             eight = incoming.at[pl.ds(0, GROUPS)]
-            pltpu.make_async_copy(eight, eight, recv_sem.at[from_slab]).wait()
-
-        got = incoming[pl.ds(GROUPS * from_slab, GROUPS)].reshape(4, 2, QUADS, 8, LANES)
+            pltpu.make_async_copy(eight, eight, recv_sem.at[before]).wait()
+
+        got = incoming[pl.ds(GROUPS * from_slab, GROUPS)]
+        third = jnp.where(late, got[:, 2], incoming[pl.ds(GROUPS * before, GROUPS), 2])
+        got = jnp.concatenate([got[:, :2], third[:, None]], axis=1).reshape(4, 2, QUADS, 8, LANES)
         a = got[:, 0].reshape(12, 8, LANES)
         b = got[:, 1].reshape(12, 8, LANES)
         near = jnp.where(half_row, a, pltpu.roll(b, 4, 1)).reshape(MEMBERS, LANES)
@@ -519,7 +563,8 @@
     returned[me] = incoming[s * GROUPS + g]
 
     halo_copy(1).wait_send()
-    halo_copy(2).wait_send()
+    back_halo.wait_send()
+    back_rates.wait_send()
     for side in range(2):
         edge_copy(side).wait_send()
         part_copy(side).wait_send()
@@ -574,8 +619,10 @@
             pltpu.VMEM((BLOCKS, OBS), i32),
             pltpu.VMEM((BLOCKS, OBS), i32),
             pltpu.VMEM((1, BLOCKS), i32),
-            pltpu.VMEM((3, PLANES, 16, 8, LANES), f32),
-            pltpu.VMEM((QUADS, STEPS, PLANES + 1, 17, 8, LANES), f32),
+            pltpu.VMEM((3, TILES, PLANES, LANES), f32),
+            pltpu.VMEM((3, PLANES + STEPS, 16, 8, LANES), f32),
+            pltpu.VMEM((2, STEPS, PLANES + 1, 17, 8, LANES), f32),
+            pltpu.VMEM((STEPS, PLANES + STEPS + 1, 17, 8, LANES), f32),
             pltpu.VMEM((DEVICES, QUADS, 8, LANES), f32),
             pltpu.VMEM((DEVICES, QUADS, 8, LANES), f32),
             pltpu.VMEM((DEVICES, QUADS, 8, LANES), f32),
@@ -590,8 +637,8 @@
             pltpu.VMEM((2, BLOCKS * MEMBERS, 2 * LANES), bf16),
             dma((QUADS,)),
             dma((7,)),
-            dma((QUADS,)),
-            dma((QUADS,)),
+            dma((4,)),
+            dma((4,)),
             dma((2,)),
             dma((2,)),
             dma((2,)),

time: 108 us -> 99 us (0.917)
  Pallas kernels: 105 us -> 96.2 us
    pallas_call x1, Pallas kernels: 105 us -> 96.2 us  [shards(): pl.pallas_call(kernel, name='analysis', out_shape=jax.ShapeDtypeStruct((m...]
where the time goes in v3:
time: 99 us; the launch traced here: 98.8 us
  Pallas kernels  96.2 us (97%)
  local copies, waits for them, and re-layouts  2.65 us (3%)
    pallas_call x1, Pallas kernels, shards(): pl.pallas_call(kernel, name='analysis', out_shape=jax.ShapeDtypeStruct((m...  96.2 us
    unnamed x1, local copies, waits for them, and re-layouts  2.65 us

profile of v3, /device:TPU:1, one launch (start us, length us, event | category | flops | bytes accessed | tf_op | source)
XLA Modules:
  0.0 98.8 jit_solution(3949936074184365456)
XLA Ops:
  0.0 96.2 %analysis.1 = f32[12,32,8,128]{3,2,1,0:T(8,128)} custom-call(f32[12,32,8,128]{3,2,1,0:T(8,128)} %bitcast.12, f32[3,32,8,128]{3,2,1,0:T(8,128)} %bitcast.13, s32[1,96]{1,0:T(1,128)} %bitcast.14, f32[4,512]{1,0:T(4,128)} %val_hbm.1, f32[4,512]{1,0:T(4,128)} %err_hbm.1, s32[4,512]{1,0:T(4,128)} %east_hbm.1, s32[4,512]{1,0:T(4,128)} %col_hbm.1, s32[1,4]{1,0:T(1,128)} %bitcast.15), custom_call_target="tpu_custom_call" | custom-call | tf_op jit(solution)/shard_map/analysis/pallas_call | solution.py:607
  96.2 2.7 %copy.10 = f32[12,8,4096]{2,1,0:T(8,128)} copy(f32[12,8,4096]{2,1,0:T(8,128)} %bitcast.11) | data formatting | bytes 3145728

commit v4 on v3

--- a/solution.py
+++ b/solution.py
@@ -143,6 +143,7 @@
     recv_sem,
     back_send,
     back_recv,
+    everyone,
 ):
     g = lax.axis_index("group")
     s = lax.axis_index("slab")
@@ -177,13 +178,20 @@
 
     barrier = pltpu.get_barrier_semaphore()
 
-    def greet(i, carry):
+    def group_peer(i):
+        return ((g + i) & (GROUPS - 1)) * SLABS + s
+
+    def slab_peer(i):
+        return g * SLABS + ((s + i) & (SLABS - 1))
+
+    for i in range(1, SLABS):
         pl.semaphore_signal(
-            barrier, inc=1, device_id=(me + i) & (DEVICES - 1), device_id_type=LOGICAL
-        )
-        return carry
-
-    lax.fori_loop(1, DEVICES, greet, 0, unroll=8)
+            barrier, inc=1, device_id=slab_peer(i), device_id_type=LOGICAL
+        )
+    for i in range(1, GROUPS):
+        pl.semaphore_signal(
+            barrier, inc=1, device_id=group_peer(i), device_id_type=LOGICAL
+        )
 
     row = iota((8, LANES), 0)
     lane = iota((8, LANES), 1)
@@ -293,16 +301,21 @@
     )
 
     grids = [state.at[0], state.at[1]]
-    for quad in range(2):
+
+    def own_cone(quad):
         take_samples(quad, grids[quad])
         for level in range(STEPS - 1):
             advance(grids[quad], level, level + 3, PLANES)
-    take_samples(2, ahead)
-
-    pl.semaphore_wait(barrier, DEVICES - 1)
+
+    own_cone(0)
+    pl.semaphore_wait(barrier, SLABS + GROUPS - 2)
     halo_copy(0).start()
     back_rates.start()
+    for i in range(1, GROUPS):
+        pl.semaphore_signal(everyone, inc=1, device_id=group_peer(i), device_id_type=LOGICAL)
+    take_samples(2, ahead)
     back_halo.start()
+    own_cone(1)
     for level in range(STEPS - 1):
         advance(ahead, level, level + 1, PLANES)
 
@@ -347,6 +360,7 @@
             device_id_type=LOGICAL,
         )
 
+    pl.semaphore_wait(everyone, GROUPS - 1)
     edge_copy(0).start()
     edge_copy(1).start()
 
@@ -365,6 +379,21 @@
     slot_order = jnp.where((member(slot_spot) == slot_lane) & (slot_spot < MEMBERS), one, zero)
     member_rows = nn(order, hot).astype(jnp.bfloat16)
     select[...] = nt(member_rows, slot_order.astype(jnp.bfloat16)).astype(jnp.bfloat16)
+
+    def send_all(quad):
+        def send(k, carry):
+            peer = (((g + (k >> 4)) & (GROUPS - 1)) * SLABS) + ((s + k) & (SLABS - 1))
+            pltpu.make_async_remote_copy(
+                src_ref=outgoing.at[peer, quad],
+                dst_ref=incoming.at[s * GROUPS + g, quad],
+                send_sem=send_sem,
+                recv_sem=recv_sem.at[s],
+                device_id=peer,
+                device_id_type=LOGICAL,
+            ).start()
+            return carry
+
+        lax.fori_loop(1, DEVICES, send, 0, unroll=2)
 
     def pack_all(quad, grid, first):
         def pack(i, carry):
@@ -396,6 +425,7 @@
     halo_copy(0).wait_send()
     halo_copy(1).start()
     forecast(0)
+    send_all(0)
     back_rates.wait_recv()
     take_rates(c_next, STEPS, PLANES)
     back_halo.wait_recv()
@@ -403,27 +433,10 @@
     for level in range(STEPS - 1):
         advance(ahead, level, PLANES, PLANES + STEPS)
     pack_all(2, ahead, STEPS)
+    send_all(2)
     forecast(1)
-
-    def each_peer(body):
-        def one(k, carry):
-            body((g + (k >> 4)) & (GROUPS - 1), (s + k) & (SLABS - 1))
-            return carry
-
-        lax.fori_loop(1, DEVICES, one, 0, unroll=2)
-
-    def send(peer_g, peer_s):
-        peer = peer_g * SLABS + peer_s
-        pltpu.make_async_remote_copy(
-            src_ref=outgoing.at[peer],
-            dst_ref=incoming.at[s * GROUPS + g],
-            send_sem=send_sem,
-            recv_sem=recv_sem.at[s],
-            device_id=peer,
-            device_id_type=LOGICAL,
-        ).start()
-
-    each_peer(send)
+    send_all(1)
+
     incoming[s * GROUPS + g] = outgoing[me]
 
     edge_copy(0).wait_recv()
@@ -647,6 +660,7 @@
             dma((SLABS,)),
             dma,
             dma,
+            pltpu.SemaphoreType.REGULAR,
         ],
         compiler_params=pltpu.CompilerParams(
             collective_id=0, has_side_effects=True, vmem_limit_bytes=56 << 20

time: 99 us -> 95.7 us (0.967)
  Pallas kernels: 96.2 us -> 92.9 us
    pallas_call x1, Pallas kernels: 96.2 us -> 92.9 us  [shards(): pl.pallas_call(kernel, name='analysis', out_shape=jax.ShapeDtypeStruct((m...]
where the time goes in v4:
time: 95.7 us; the launch traced here: 95.6 us
  Pallas kernels  92.9 us (97%)
  local copies, waits for them, and re-layouts  2.65 us (3%)
    pallas_call x1, Pallas kernels, shards(): pl.pallas_call(kernel, name='analysis', out_shape=jax.ShapeDtypeStruct((m...  92.9 us
    unnamed x1, local copies, waits for them, and re-layouts  2.65 us

profile of v4, /device:TPU:1, one launch (start us, length us, event | category | flops | bytes accessed | tf_op | source)
XLA Modules:
  0.0 95.6 jit_solution(14084444849319387876)
XLA Ops:
  0.0 92.9 %analysis.1 = f32[12,32,8,128]{3,2,1,0:T(8,128)} custom-call(f32[12,32,8,128]{3,2,1,0:T(8,128)} %bitcast.12, f32[3,32,8,128]{3,2,1,0:T(8,128)} %bitcast.13, s32[1,96]{1,0:T(1,128)} %bitcast.14, f32[4,512]{1,0:T(4,128)} %val_hbm.1, f32[4,512]{1,0:T(4,128)} %err_hbm.1, s32[4,512]{1,0:T(4,128)} %east_hbm.1, s32[4,512]{1,0:T(4,128)} %col_hbm.1, s32[1,4]{1,0:T(1,128)} %bitcast.15), custom_call_target="tpu_custom_call" | custom-call | tf_op jit(solution)/shard_map/analysis/pallas_call | solution.py:620
  92.9 2.7 %copy.10 = f32[12,8,4096]{2,1,0:T(8,128)} copy(f32[12,8,4096]{2,1,0:T(8,128)} %bitcast.11) | data formatting | bytes 3145728

commit v5 on v4

--- a/solution.py
+++ b/solution.py
@@ -40,12 +40,18 @@
     return high, (a - high.astype(jnp.float32)).astype(jnp.bfloat16)
 
 
+def padded(a):
+    return jnp.concatenate([a, jnp.zeros((LANES - MEMBERS, LANES), a.dtype)], axis=0)
+
+
 def product(a, b):
-    m = a.shape[0]
     ah, al = halves(a)
     bh, bl = halves(b)
-    both = nn(jnp.concatenate([ah, al], axis=0), jnp.concatenate([bh, bl], axis=1))
-    return both[:m, :LANES] + (both[:m, LANES:] + both[m:, :LANES])
+    bh, bl = padded(bh), padded(bl)
+    top = jnp.concatenate([bh, bl], axis=1)
+    bottom = jnp.concatenate([bh, jnp.zeros_like(bl)], axis=1)
+    both = nn(jnp.concatenate([ah, al], axis=1), jnp.concatenate([top, bottom], axis=0))
+    return both[:, :LANES] + both[:, LANES:]
 
 
 def swap_rows(tiles, row):
@@ -140,6 +146,7 @@
     part_send,
     part_recv,
     send_sem,
+    early_sem,
     recv_sem,
     back_send,
     back_recv,
@@ -273,32 +280,46 @@
     next_slab = g * SLABS + ((s + 1) & (SLABS - 1))
     last_slab = g * SLABS + ((s + SLABS - 1) & (SLABS - 1))
 
-    def halo_copy(quad):
+    def halo_copy(quad, low, high, sem):
+        levels = pl.ds(low, high - low)
         return pltpu.make_async_remote_copy(
-            src_ref=state.at[quad, :, PLANES, pl.ds(1, 16)],
-            dst_ref=state.at[quad, :, 0, pl.ds(1, 16)],
-            send_sem=halo_send.at[quad],
-            recv_sem=halo_recv.at[quad],
+            src_ref=state.at[quad, levels, PLANES, pl.ds(1, 16)],
+            dst_ref=state.at[quad, levels, 0, pl.ds(1, 16)],
+            send_sem=halo_send.at[sem],
+            recv_sem=halo_recv.at[sem],
             device_id=next_slab,
             device_id_type=LOGICAL,
         )
+
+    halo_0 = halo_copy(0, 0, STEPS, 0)
+    halo_1a = halo_copy(1, 0, 3, 1)
+    halo_1b = halo_copy(1, 3, STEPS, 2)
 
     back_halo = pltpu.make_async_remote_copy(
         src_ref=ahead.at[0, pl.ds(1, STEPS), pl.ds(1, 16)],
         dst_ref=ahead.at[0, pl.ds(PLANES + 1, STEPS), pl.ds(1, 16)],
-        send_sem=halo_send.at[2],
-        recv_sem=halo_recv.at[2],
-        device_id=last_slab,
-        device_id_type=LOGICAL,
-    )
-    back_rates = pltpu.make_async_remote_copy(
-        src_ref=c_ref,
-        dst_ref=c_next,
         send_sem=halo_send.at[3],
         recv_sem=halo_recv.at[3],
         device_id=last_slab,
         device_id_type=LOGICAL,
     )
+    half = pl.ds((g & 1) * (TILES // 2), TILES // 2)
+    back_rates = pltpu.make_async_remote_copy(
+        src_ref=c_ref.at[:, half],
+        dst_ref=c_next.at[:, half],
+        send_sem=halo_send.at[4],
+        recv_sem=halo_recv.at[4],
+        device_id=last_slab,
+        device_id_type=LOGICAL,
+    )
+    share_rates = pltpu.make_async_remote_copy(
+        src_ref=c_next.at[:, half],
+        dst_ref=c_next.at[:, half],
+        send_sem=halo_send.at[5],
+        recv_sem=halo_recv.at[5],
+        device_id=(g ^ 1) * SLABS + s,
+        device_id_type=LOGICAL,
+    )
 
     grids = [state.at[0], state.at[1]]
 
@@ -309,15 +330,18 @@
 
     own_cone(0)
     pl.semaphore_wait(barrier, SLABS + GROUPS - 2)
-    halo_copy(0).start()
+    halo_0.start()
     back_rates.start()
     for i in range(1, GROUPS):
         pl.semaphore_signal(everyone, inc=1, device_id=group_peer(i), device_id_type=LOGICAL)
     take_samples(2, ahead)
     back_halo.start()
     own_cone(1)
+    halo_1a.start()
     for level in range(STEPS - 1):
         advance(ahead, level, level + 1, PLANES)
+    back_rates.wait_recv()
+    share_rates.start()
 
     for copy in small_copies:
         copy.wait()
@@ -386,14 +410,33 @@
             pltpu.make_async_remote_copy(
                 src_ref=outgoing.at[peer, quad],
                 dst_ref=incoming.at[s * GROUPS + g, quad],
-                send_sem=send_sem,
-                recv_sem=recv_sem.at[s],
+                send_sem=send_sem.at[quad],
+                recv_sem=early_sem.at[quad],
                 device_id=peer,
                 device_id_type=LOGICAL,
             ).start()
             return carry
 
         lax.fori_loop(1, DEVICES, send, 0, unroll=2)
+
+    def slab_of(i, c, sign):
+        z = (s >> 2) + sign * (c + i)
+        y = s + sign * c
+        return ((z & 3) << 2) | (y & 3)
+
+    def send_last(k, carry):
+        peer_g = (g + (k >> 2) + 2 * k) & (GROUPS - 1)
+        peer_s = slab_of(k >> 5, k & 3, 1)
+        peer = peer_g * SLABS + peer_s
+        pltpu.make_async_remote_copy(
+            src_ref=outgoing.at[peer, 1],
+            dst_ref=incoming.at[s * GROUPS + g, 1],
+            send_sem=send_sem.at[1],
+            recv_sem=recv_sem.at[s],
+            device_id=peer,
+            device_id_type=LOGICAL,
+        ).start()
+        return carry
 
     def pack_all(quad, grid, first):
         def pack(i, carry):
@@ -416,17 +459,14 @@
 
         lax.fori_loop(0, 4, pack, 0)
 
-    def forecast(quad):
-        halo_copy(quad).wait_recv()
-        for level in range(STEPS - 1):
-            advance(grids[quad], level, 0, level + 3)
-        pack_all(quad, grids[quad], 0)
-
-    halo_copy(0).wait_send()
-    halo_copy(1).start()
-    forecast(0)
+    halo_0.wait_send()
+    halo_1b.start()
+    halo_0.wait_recv()
+    for level in range(STEPS - 1):
+        advance(grids[0], level, 0, level + 3)
+    pack_all(0, grids[0], 0)
     send_all(0)
-    back_rates.wait_recv()
+    share_rates.wait_recv()
     take_rates(c_next, STEPS, PLANES)
     back_halo.wait_recv()
     wrap(ahead, 0, PLANES, PLANES + STEPS)
@@ -434,9 +474,14 @@
         advance(ahead, level, PLANES, PLANES + STEPS)
     pack_all(2, ahead, STEPS)
     send_all(2)
-    forecast(1)
-    send_all(1)
-
+    halo_1a.wait_recv()
+    for level in range(3):
+        advance(grids[1], level, 0, level + 3)
+    halo_1b.wait_recv()
+    for level in range(3, STEPS - 1):
+        advance(grids[1], level, 0, level + 3)
+    pack_all(1, grids[1], 0)
+    lax.fori_loop(1, DEVICES, send_last, 0, unroll=2)
     incoming[s * GROUPS + g] = outgoing[me]
 
     edge_copy(0).wait_recv()
@@ -449,46 +494,58 @@
     pad = jnp.zeros((LANES - MEMBERS, CELLS), jnp.bfloat16)
 
     late = (iota((GROUPS, 8, LANES), 1) >= 4) & (iota((GROUPS, 8, LANES), 2) >= 64)
-    seven = incoming.at[pl.ds(0, GROUPS - 1)]
+    for quad in (0, 2):
+        most = incoming.at[pl.ds(0, DEVICES - 1), quad]
+        pltpu.make_async_copy(most, most, early_sem.at[quad]).wait()
+    seven = incoming.at[pl.ds(0, GROUPS - 1), 1]
     pltpu.make_async_copy(seven, seven, recv_sem.at[s]).wait()
 
     def gather(i, carry):
-        from_slab = (s - i) & (SLABS - 1)
-        before = (s - i - 1) & (SLABS - 1)
-
-        @pl.when(i < SLABS - 1)
+        slabs = [slab_of(i >> 1, 2 * (i & 1) + k, -1) for k in range(2)]
+        eight = incoming.at[pl.ds(0, GROUPS), 1]
+
+        @pl.when(i > 0)
         def _():
-            eight = incoming.at[pl.ds(0, GROUPS)]
-            pltpu.make_async_copy(eight, eight, recv_sem.at[before]).wait()
-
-        got = incoming[pl.ds(GROUPS * from_slab, GROUPS)]
-        third = jnp.where(late, got[:, 2], incoming[pl.ds(GROUPS * before, GROUPS), 2])
-        got = jnp.concatenate([got[:, :2], third[:, None]], axis=1).reshape(4, 2, QUADS, 8, LANES)
-        a = got[:, 0].reshape(12, 8, LANES)
-        b = got[:, 1].reshape(12, 8, LANES)
-        near = jnp.where(half_row, a, pltpu.roll(b, 4, 1)).reshape(MEMBERS, LANES)
-        far = jnp.where(half_row, pltpu.roll(a, 4, 1), b).reshape(MEMBERS, LANES)
-        field = jnp.concatenate([near, far], axis=1)
-        mean = jnp.sum(field, axis=0, keepdims=True) * (1.0 / MEMBERS)
-        mean_of[from_slab] = mean
-        away = field - mean
-        high, low = halves(away)
-        right_side = jnp.concatenate([high, pad, low, pad], axis=0)
-        split[from_slab] = right_side
-        pieces = []
-        for b in range(BLOCKS + 2):
-            omega = maps[b, pl.ds(from_slab, 1)]
-            v = maps[b, pl.ds(SLABS + from_slab, 1)]
-            pieces.append(omega * away)
-            pieces.append(jnp.broadcast_to(v - mean * omega, (ROWS - MEMBERS, CELLS)))
-        lhs_high, lhs_low = halves(jnp.concatenate(pieces, axis=0))
-        high_part = nt(lhs_high, right_side)
-        low_part = nt(lhs_low, right_side[:LANES])
+            pltpu.make_async_copy(eight, eight, recv_sem.at[slabs[0]]).wait()
+
+        pltpu.make_async_copy(eight, eight, recv_sem.at[slabs[1]]).wait()
+        highs, lows, sides = [], [], []
+        for k in range(2):
+            from_slab = slabs[k]
+            before = (from_slab - 1) & (SLABS - 1)
+            got = incoming[pl.ds(GROUPS * from_slab, GROUPS)]
+            third = jnp.where(late, got[:, 2], incoming[pl.ds(GROUPS * before, GROUPS), 2])
+            got = jnp.concatenate([got[:, :2], third[:, None]], axis=1)
+            got = got.reshape(4, 2, QUADS, 8, LANES)
+            a = got[:, 0].reshape(12, 8, LANES)
+            b = got[:, 1].reshape(12, 8, LANES)
+            near = jnp.where(half_row, a, pltpu.roll(b, 4, 1)).reshape(MEMBERS, LANES)
+            far = jnp.where(half_row, pltpu.roll(a, 4, 1), b).reshape(MEMBERS, LANES)
+            field = jnp.concatenate([near, far], axis=1)
+            mean = jnp.sum(field, axis=0, keepdims=True) * (1.0 / MEMBERS)
+            mean_of[from_slab] = mean
+            away = field - mean
+            high, low = halves(away)
+            right_side = jnp.concatenate([high, pad, low, pad], axis=0)
+            split[from_slab] = right_side
+            pieces = []
+            for b in range(BLOCKS + 2):
+                omega = maps[b, pl.ds(from_slab, 1)]
+                v = maps[b, pl.ds(SLABS + from_slab, 1)]
+                pieces.append(omega * away)
+                pieces.append(jnp.broadcast_to(v - mean * omega, (ROWS - MEMBERS, CELLS)))
+            lhs_high, lhs_low = halves(jnp.concatenate(pieces, axis=0))
+            highs.append(lhs_high)
+            lows.append(lhs_low)
+            sides.append(right_side)
+        side = jnp.concatenate(sides, axis=1)
+        high_part = nt(jnp.concatenate(highs, axis=1), side)
+        low_part = nt(jnp.concatenate(lows, axis=1), side[:LANES])
         total = high_part[:, :LANES] + high_part[:, LANES:] + low_part
         acc[...] += total.reshape(acc.shape)
         return carry
 
-    lax.fori_loop(0, SLABS, gather, 0)
+    lax.fori_loop(0, SLABS // 2, gather, 0)
 
     def part_copy(side):
         return pltpu.make_async_remote_copy(
@@ -503,14 +560,13 @@
     part_copy(0).start()
     part_copy(1).start()
 
-    identity = jnp.where((spot == across) & (spot < MEMBERS), one, zero)
-    empty = jnp.zeros((LANES - MEMBERS, LANES), jnp.float32)
+    identity = jnp.where((spot == across) & (spot < MEMBERS), one, zero)[:MEMBERS]
     part_copy(0).wait_recv()
     part_copy(1).wait_recv()
     totals = [acc[b] for b in range(BLOCKS)]
     totals[BLOCKS - 1] = totals[BLOCKS - 1] + part_in[0]
     totals[0] = totals[0] + part_in[1]
-    grams = [identity + jnp.concatenate([t[:MEMBERS], empty], axis=0) for t in totals]
+    grams = [identity + t[:MEMBERS] for t in totals]
     fros = [jnp.sqrt(jnp.sum(t * t, keepdims=True)) for t in grams]
     a_of = [t / f for t, f in zip(grams, fros)]
     middles = [1.5 * identity - 0.5 * a for a in a_of]
@@ -526,58 +582,65 @@
         projected = jnp.broadcast_to(totals[b][MEMBERS : MEMBERS + 1], (16, LANES))
         mean_weights = product(product(projected, transform), transform)[:1]
         high, low = halves(transform)
-        both = nn(select[...], jnp.concatenate([high, low], axis=1))
+        both = nn(select[...], jnp.concatenate([padded(high), padded(low)], axis=1))
         by_member = (both[:MEMBERS, :LANES] + both[:MEMBERS, LANES:]) + mean_weights
         high, low = halves(by_member)
         ordered[0, MEMBERS * b : MEMBERS * (b + 1)] = jnp.concatenate([high, high], axis=1)
         ordered[1, MEMBERS * b : MEMBERS * (b + 1)] = jnp.concatenate([low, low], axis=1)
 
-    all_but_one = outgoing.at[pl.ds(0, DEVICES - 1)]
-    pltpu.make_async_copy(all_but_one, all_but_one, send_sem).wait()
+    for quad in range(QUADS):
+        most = outgoing.at[pl.ds(0, DEVICES - 1), quad]
+        pltpu.make_async_copy(most, most, send_sem.at[quad]).wait()
 
     block_of = (iota((MEMBERS, CELLS), 1) % OWN) // TILE_WIDTH
 
     def give_back(i, carry):
-        to_slab = (s + i) % SLABS
-        right_side = split[to_slab]
-        parts = nn(ordered[0], right_side) + nn(ordered[1], right_side)
-        field = parts[:MEMBERS]
-        for b in range(1, BLOCKS):
-            field = jnp.where(block_of == b, parts[MEMBERS * b : MEMBERS * (b + 1)], field)
-        field = field + mean_of[to_slab]
-        near = field[:, :LANES].reshape(12, 8, LANES)
-        far = field[:, LANES:].reshape(12, 8, LANES)
-        even = jnp.where(half_row, near, pltpu.roll(far, 4, 1)).reshape(4, QUADS, 8, LANES)
-        odd = jnp.where(half_row, pltpu.roll(near, 4, 1), far).reshape(4, QUADS, 8, LANES)
-        for a in range(4):
-            incoming[GROUPS * to_slab + 2 * a] = even[a]
-            incoming[GROUPS * to_slab + 2 * a + 1] = odd[a]
+        to_slabs = []
+        for c in range(4):
+            to_slab = slab_of(i, c, 1)
+            to_slabs.append(to_slab)
+            right_side = split[to_slab]
+            parts = nn(ordered[0], right_side) + nn(ordered[1], right_side)
+            field = parts[:MEMBERS]
+            for b in range(1, BLOCKS):
+                field = jnp.where(block_of == b, parts[MEMBERS * b : MEMBERS * (b + 1)], field)
+            field = field + mean_of[to_slab]
+            near = field[:, :LANES].reshape(12, 8, LANES)
+            far = field[:, LANES:].reshape(12, 8, LANES)
+            even = jnp.where(half_row, near, pltpu.roll(far, 4, 1)).reshape(4, QUADS, 8, LANES)
+            odd = jnp.where(half_row, pltpu.roll(near, 4, 1), far).reshape(4, QUADS, 8, LANES)
+            for a in range(4):
+                incoming[GROUPS * to_slab + 2 * a] = even[a]
+                incoming[GROUPS * to_slab + 2 * a + 1] = odd[a]
 
         def to_group(j, carry):
-            peer_g = (g + j) & (GROUPS - 1)
-
-            @pl.when(i * GROUPS + j > 0)
-            def _():
-                pltpu.make_async_remote_copy(
-                    src_ref=incoming.at[GROUPS * to_slab + peer_g],
-                    dst_ref=returned.at[me],
-                    send_sem=back_send,
-                    recv_sem=back_recv,
-                    device_id=peer_g * SLABS + to_slab,
-                    device_id_type=LOGICAL,
-                ).start()
-
+            for c in range(4):
+                peer_g = (g + j + 2 * c) & (GROUPS - 1)
+
+                def start():
+                    pltpu.make_async_remote_copy(
+                        src_ref=incoming.at[GROUPS * to_slabs[c] + peer_g],
+                        dst_ref=returned.at[me],
+                        send_sem=back_send,
+                        recv_sem=back_recv,
+                        device_id=peer_g * SLABS + to_slabs[c],
+                        device_id_type=LOGICAL,
+                    ).start()
+
+                if c == 0:
+                    pl.when(i * GROUPS + j > 0)(start)
+                else:
+                    start()
             return carry
 
         lax.fori_loop(0, GROUPS, to_group, 0)
         return carry
 
-    lax.fori_loop(0, SLABS, give_back, 0)
+    lax.fori_loop(0, 4, give_back, 0)
     returned[me] = incoming[s * GROUPS + g]
 
-    halo_copy(1).wait_send()
-    back_halo.wait_send()
-    back_rates.wait_send()
+    for copy in (halo_1a, halo_1b, back_halo, back_rates, share_rates):
+        copy.wait_send()
     for side in range(2):
         edge_copy(side).wait_send()
         part_copy(side).wait_send()
@@ -594,7 +657,7 @@
                 o_ref[4 * quad + i, tile] = tiles[i]
         return carry
 
-    lax.fori_loop(0, TILES, unpack, 0, unroll=2)
+    lax.fori_loop(0, TILES, unpack, 0, unroll=4)
 
 
 def shards(
@@ -650,13 +713,14 @@
             pltpu.VMEM((2, BLOCKS * MEMBERS, 2 * LANES), bf16),
             dma((QUADS,)),
             dma((7,)),
-            dma((4,)),
-            dma((4,)),
+            dma((6,)),
+            dma((6,)),
             dma((2,)),
             dma((2,)),
             dma((2,)),
             dma((2,)),
-            dma,
+            dma((QUADS,)),
+            dma((QUADS,)),
             dma((SLABS,)),
             dma,
             dma,

time: 95.7 us -> 88.2 us (0.922)
  Pallas kernels: 92.9 us -> 85.4 us
    pallas_call x1, Pallas kernels: 92.9 us -> 85.4 us  [shards(): pl.pallas_call(kernel, name='analysis', out_shape=jax.ShapeDtypeStruct((m...]
where the time goes in v5:
time: 88.2 us; the launch traced here: 88.1 us
  Pallas kernels  85.4 us (97%)
  local copies, waits for them, and re-layouts  2.65 us (3%)
    pallas_call x1, Pallas kernels, shards(): pl.pallas_call(kernel, name='analysis', out_shape=jax.ShapeDtypeStruct((m...  85.4 us
    unnamed x1, local copies, waits for them, and re-layouts  2.65 us

profile of v5, /device:TPU:1, one launch (start us, length us, event | category | flops | bytes accessed | tf_op | source)
XLA Modules:
  0.0 88.1 jit_solution(9311990582595711656)
XLA Ops:
  0.0 85.4 %analysis.1 = f32[12,32,8,128]{3,2,1,0:T(8,128)} custom-call(f32[12,32,8,128]{3,2,1,0:T(8,128)} %bitcast.12, f32[3,32,8,128]{3,2,1,0:T(8,128)} %bitcast.13, s32[1,96]{1,0:T(1,128)} %bitcast.14, f32[4,512]{1,0:T(4,128)} %val_hbm.1, f32[4,512]{1,0:T(4,128)} %err_hbm.1, s32[4,512]{1,0:T(4,128)} %east_hbm.1, s32[4,512]{1,0:T(4,128)} %col_hbm.1, s32[1,4]{1,0:T(1,128)} %bitcast.15), custom_call_target="tpu_custom_call" | custom-call | tf_op jit(solution)/shard_map/analysis/pallas_call | solution.py:683
  85.4 2.7 %copy.10 = f32[12,8,4096]{2,1,0:T(8,128)} copy(f32[12,8,4096]{2,1,0:T(8,128)} %bitcast.11) | data formatting | bytes 3145728

commit v6 on v5

--- a/solution.py
+++ b/solution.py
@@ -267,7 +267,7 @@
 
     def advance(grid, level, first, end):
         planes = end - first
-        n = 16 if planes < 3 else 8 if planes < 6 else 4
+        n = 16 if planes < 4 else 8
 
         def one(i, carry):
             new = stepped(grid, level, first, end, n * i, n)
@@ -291,7 +291,8 @@
             device_id_type=LOGICAL,
         )
 
-    halo_0 = halo_copy(0, 0, STEPS, 0)
+    halo_0a = halo_copy(0, 0, 3, 0)
+    halo_0b = halo_copy(0, 3, STEPS, 6)
     halo_1a = halo_copy(1, 0, 3, 1)
     halo_1b = halo_copy(1, 3, STEPS, 2)
 
@@ -328,10 +329,15 @@
         for level in range(STEPS - 1):
             advance(grids[quad], level, level + 3, PLANES)
 
-    own_cone(0)
+    take_samples(0, grids[0])
+    for level in range(2):
+        advance(grids[0], level, level + 3, PLANES)
     pl.semaphore_wait(barrier, SLABS + GROUPS - 2)
-    halo_0.start()
+    halo_0a.start()
     back_rates.start()
+    for level in range(2, STEPS - 1):
+        advance(grids[0], level, level + 3, PLANES)
+    halo_0b.start()
     for i in range(1, GROUPS):
         pl.semaphore_signal(everyone, inc=1, device_id=group_peer(i), device_id_type=LOGICAL)
     take_samples(2, ahead)
@@ -459,13 +465,15 @@
 
         lax.fori_loop(0, 4, pack, 0)
 
-    halo_0.wait_send()
+    halo_0b.wait_send()
     halo_1b.start()
-    halo_0.wait_recv()
-    for level in range(STEPS - 1):
+    halo_0a.wait_recv()
+    for level in range(3):
+        advance(grids[0], level, 0, level + 3)
+    halo_0b.wait_recv()
+    for level in range(3, STEPS - 1):
         advance(grids[0], level, 0, level + 3)
     pack_all(0, grids[0], 0)
-    send_all(0)
     share_rates.wait_recv()
     take_rates(c_next, STEPS, PLANES)
     back_halo.wait_recv()
@@ -473,6 +481,7 @@
     for level in range(STEPS - 1):
         advance(ahead, level, PLANES, PLANES + STEPS)
     pack_all(2, ahead, STEPS)
+    send_all(0)
     send_all(2)
     halo_1a.wait_recv()
     for level in range(3):
@@ -639,7 +648,7 @@
     lax.fori_loop(0, 4, give_back, 0)
     returned[me] = incoming[s * GROUPS + g]
 
-    for copy in (halo_1a, halo_1b, back_halo, back_rates, share_rates):
+    for copy in (halo_0a, halo_1a, halo_1b, back_halo, back_rates, share_rates):
         copy.wait_send()
     for side in range(2):
         edge_copy(side).wait_send()
@@ -713,8 +722,8 @@
             pltpu.VMEM((2, BLOCKS * MEMBERS, 2 * LANES), bf16),
             dma((QUADS,)),
             dma((7,)),
-            dma((6,)),
-            dma((6,)),
+            dma((7,)),
+            dma((7,)),
             dma((2,)),
             dma((2,)),
             dma((2,)),

time: 88.2 us -> 86.4 us (0.980)
  Pallas kernels: 85.4 us -> 83 us
    pallas_call x1, Pallas kernels: 85.4 us -> 83 us  [shards(): pl.pallas_call(kernel, name='analysis', out_shape=jax.ShapeDtypeStruct((m...]
where the time goes in v6:
time: 86.4 us; the launch traced here: 85.6 us
  Pallas kernels  83 us (96%)
  local copies, waits for them, and re-layouts  2.65 us (3%)
    pallas_call x1, Pallas kernels, shards(): pl.pallas_call(kernel, name='analysis', out_shape=jax.ShapeDtypeStruct((m...  83 us
    unnamed x1, local copies, waits for them, and re-layouts  2.65 us

profile of v6, /device:TPU:1, one launch (start us, length us, event | category | flops | bytes accessed | tf_op | source)
XLA Modules:
  0.0 85.6 jit_solution(17788433275343191788)
XLA Ops:
  0.0 83.0 %analysis.1 = f32[12,32,8,128]{3,2,1,0:T(8,128)} custom-call(f32[12,32,8,128]{3,2,1,0:T(8,128)} %bitcast.12, f32[3,32,8,128]{3,2,1,0:T(8,128)} %bitcast.13, s32[1,96]{1,0:T(1,128)} %bitcast.14, f32[4,512]{1,0:T(4,128)} %val_hbm.1, f32[4,512]{1,0:T(4,128)} %err_hbm.1, s32[4,512]{1,0:T(4,128)} %east_hbm.1, s32[4,512]{1,0:T(4,128)} %col_hbm.1, s32[1,4]{1,0:T(1,128)} %bitcast.15), custom_call_target="tpu_custom_call" | custom-call | tf_op jit(solution)/shard_map/analysis/pallas_call | solution.py:692
  83.0 2.7 %copy.10 = f32[12,8,4096]{2,1,0:T(8,128)} copy(f32[12,8,4096]{2,1,0:T(8,128)} %bitcast.11) | data formatting | bytes 3145728

commit v7 on v6

--- a/solution.py
+++ b/solution.py
@@ -398,7 +398,7 @@
     across = iota((LANES, LANES), 1)
 
     def member(r):
-        return 24 * (r // 24) + 12 * ((r // 4) % 2) + 4 * ((r // 8) % 3) + r % 4
+        return 24 * (r // 24) + 12 * ((r // 4) % 2) + 4 * (2 * ((r // 8) % 3) % 3) + r % 4
 
     one = jnp.float32(1.0)
     zero = jnp.float32(0.0)
@@ -410,14 +410,16 @@
     member_rows = nn(order, hot).astype(jnp.bfloat16)
     select[...] = nt(member_rows, slot_order.astype(jnp.bfloat16)).astype(jnp.bfloat16)
 
-    def send_all(quad):
+    early = pl.ds(0, 2)
+
+    def send_early():
         def send(k, carry):
             peer = (((g + (k >> 4)) & (GROUPS - 1)) * SLABS) + ((s + k) & (SLABS - 1))
             pltpu.make_async_remote_copy(
-                src_ref=outgoing.at[peer, quad],
-                dst_ref=incoming.at[s * GROUPS + g, quad],
-                send_sem=send_sem.at[quad],
-                recv_sem=early_sem.at[quad],
+                src_ref=outgoing.at[peer, early],
+                dst_ref=incoming.at[s * GROUPS + g, early],
+                send_sem=send_sem.at[0],
+                recv_sem=early_sem,
                 device_id=peer,
                 device_id_type=LOGICAL,
             ).start()
@@ -435,8 +437,8 @@
         peer_s = slab_of(k >> 5, k & 3, 1)
         peer = peer_g * SLABS + peer_s
         pltpu.make_async_remote_copy(
-            src_ref=outgoing.at[peer, 1],
-            dst_ref=incoming.at[s * GROUPS + g, 1],
+            src_ref=outgoing.at[peer, 2],
+            dst_ref=incoming.at[s * GROUPS + g, 2],
             send_sem=send_sem.at[1],
             recv_sem=recv_sem.at[s],
             device_id=peer,
@@ -444,7 +446,7 @@
         ).start()
         return carry
 
-    def pack_all(quad, grid, first):
+    def pack_all(slot, grid, first):
         def pack(i, carry):
             ty = 4 * i
             new = stepped(grid, STEPS - 1, first, first + PLANES, ty, 4)
@@ -460,7 +462,7 @@
                 for j, tile in enumerate(swap_lanes(tiles, lane)):
                     for k in range(4):
                         at = 64 * h + 32 * (j // 2) + 2 * k + j % 2
-                        outgoing[at + 2 * ty, quad] = tile[k]
+                        outgoing[at + 2 * ty, slot] = tile[k]
             return carry
 
         lax.fori_loop(0, 4, pack, 0)
@@ -480,16 +482,15 @@
     wrap(ahead, 0, PLANES, PLANES + STEPS)
     for level in range(STEPS - 1):
         advance(ahead, level, PLANES, PLANES + STEPS)
-    pack_all(2, ahead, STEPS)
-    send_all(0)
-    send_all(2)
+    pack_all(1, ahead, STEPS)
+    send_early()
     halo_1a.wait_recv()
     for level in range(3):
         advance(grids[1], level, 0, level + 3)
     halo_1b.wait_recv()
     for level in range(3, STEPS - 1):
         advance(grids[1], level, 0, level + 3)
-    pack_all(1, grids[1], 0)
+    pack_all(2, grids[1], 0)
     lax.fori_loop(1, DEVICES, send_last, 0, unroll=2)
     incoming[s * GROUPS + g] = outgoing[me]
 
@@ -503,15 +504,14 @@
     pad = jnp.zeros((LANES - MEMBERS, CELLS), jnp.bfloat16)
 
     late = (iota((GROUPS, 8, LANES), 1) >= 4) & (iota((GROUPS, 8, LANES), 2) >= 64)
-    for quad in (0, 2):
-        most = incoming.at[pl.ds(0, DEVICES - 1), quad]
-        pltpu.make_async_copy(most, most, early_sem.at[quad]).wait()
-    seven = incoming.at[pl.ds(0, GROUPS - 1), 1]
+    most = incoming.at[pl.ds(0, DEVICES - 1), early]
+    pltpu.make_async_copy(most, most, early_sem).wait()
+    seven = incoming.at[pl.ds(0, GROUPS - 1), 2]
     pltpu.make_async_copy(seven, seven, recv_sem.at[s]).wait()
 
     def gather(i, carry):
         slabs = [slab_of(i >> 1, 2 * (i & 1) + k, -1) for k in range(2)]
-        eight = incoming.at[pl.ds(0, GROUPS), 1]
+        eight = incoming.at[pl.ds(0, GROUPS), 2]
 
         @pl.when(i > 0)
         def _():
@@ -523,8 +523,8 @@
             from_slab = slabs[k]
             before = (from_slab - 1) & (SLABS - 1)
             got = incoming[pl.ds(GROUPS * from_slab, GROUPS)]
-            third = jnp.where(late, got[:, 2], incoming[pl.ds(GROUPS * before, GROUPS), 2])
-            got = jnp.concatenate([got[:, :2], third[:, None]], axis=1)
+            ahead_of = jnp.where(late, got[:, 1], incoming[pl.ds(GROUPS * before, GROUPS), 1])
+            got = jnp.concatenate([got[:, :1], ahead_of[:, None], got[:, 2:]], axis=1)
             got = got.reshape(4, 2, QUADS, 8, LANES)
             a = got[:, 0].reshape(12, 8, LANES)
             b = got[:, 1].reshape(12, 8, LANES)
@@ -597,9 +597,9 @@
         ordered[0, MEMBERS * b : MEMBERS * (b + 1)] = jnp.concatenate([high, high], axis=1)
         ordered[1, MEMBERS * b : MEMBERS * (b + 1)] = jnp.concatenate([low, low], axis=1)
 
-    for quad in range(QUADS):
-        most = outgoing.at[pl.ds(0, DEVICES - 1), quad]
-        pltpu.make_async_copy(most, most, send_sem.at[quad]).wait()
+    for i, part in enumerate((early, 2)):
+        most = outgoing.at[pl.ds(0, DEVICES - 1), part]
+        pltpu.make_async_copy(most, most, send_sem.at[i]).wait()
 
     block_of = (iota((MEMBERS, CELLS), 1) % OWN) // TILE_WIDTH
 
@@ -663,7 +663,7 @@
             tiles = swap_lanes([returned[4 * tile + q, quad] for q in range(4)], lane)
             tiles = swap_rows(tiles, row)
             for i in range(4):
-                o_ref[4 * quad + i, tile] = tiles[i]
+                o_ref[4 * (2 * quad % 3) + i, tile] = tiles[i]
         return carry
 
     lax.fori_loop(0, TILES, unpack, 0, unroll=4)
@@ -728,8 +728,8 @@
             dma((2,)),
             dma((2,)),
             dma((2,)),
-            dma((QUADS,)),
-            dma((QUADS,)),
+            dma((2,)),
+            dma,
             dma((SLABS,)),
             dma,
             dma,

time: 86.4 us -> 86.2 us (level)
  no operation moved by 1% of the time
where the time goes in v7:
time: 86.2 us; the launch traced here: 85.5 us
  Pallas kernels  82.8 us (96%)
  local copies, waits for them, and re-layouts  2.65 us (3%)
    pallas_call x1, Pallas kernels, shards(): pl.pallas_call(kernel, name='analysis', out_shape=jax.ShapeDtypeStruct((m...  82.8 us
    unnamed x1, local copies, waits for them, and re-layouts  2.65 us

profile of v7, /device:TPU:1, one launch (start us, length us, event | category | flops | bytes accessed | tf_op | source)
XLA Modules:
  0.0 85.5 jit_solution(18393078518156013962)
XLA Ops:
  0.0 82.8 %analysis.1 = f32[12,32,8,128]{3,2,1,0:T(8,128)} custom-call(f32[12,32,8,128]{3,2,1,0:T(8,128)} %bitcast.12, f32[3,32,8,128]{3,2,1,0:T(8,128)} %bitcast.13, s32[1,96]{1,0:T(1,128)} %bitcast.14, f32[4,512]{1,0:T(4,128)} %val_hbm.1, f32[4,512]{1,0:T(4,128)} %err_hbm.1, s32[4,512]{1,0:T(4,128)} %east_hbm.1, s32[4,512]{1,0:T(4,128)} %col_hbm.1, s32[1,4]{1,0:T(1,128)} %bitcast.15), custom_call_target="tpu_custom_call" | custom-call | tf_op jit(solution)/shard_map/analysis/pallas_call | solution.py:692
  82.8 2.7 %copy.10 = f32[12,8,4096]{2,1,0:T(8,128)} copy(f32[12,8,4096]{2,1,0:T(8,128)} %bitcast.11) | data formatting | bytes 3145728
